TPU v7x, 32 devices: a whole 2x2x4 slice. The times are simulated.
32 devices in a mesh: row: 4 (over y, core), col: 8 (over z, x).
Axes of the slice: x: 2, y: 2, z: 4, core: 2. Of those that a mesh axis runs over, the one named last changes fastest.
Arguments:
- resid_deriv: bfloat16 [256, 512, 1024], P(('row', 'col')), may hold values from -0.03125 to 0.03125
- local_deriv: bfloat16 [256, 512, 128], P(('row', 'col'))
- inv_factor: float32 [256, 128, 128], P(('row', 'col'))
- block_ids: int32 [256, 8], P(('row', 'col')), may hold values from 0 to 31, as said below
- right_sides: float32 [4096, 256], P(('col', 'row')), may hold values from -6 to 6
- damping: float32 [4096], P(('col', 'row')), may hold values from 0.25 to 2
Outputs:
- normal: float32 [8, 4, 128, 4096], P(None, 'row', None, 'col')
- solution: float32 [4096, 256], P(('col', 'row'))
Inputs may be any that keep to these rules, and one draw needn't show every extreme that they name: `block_ids`: all 8 bundles in each aligned block of 8 rows name the same 8 distinct blocks, each bundle in its own order. Among one such set, the values block // 4 are distinct and every residue block % 4 appears exactly 2 times.
All inputs are finite; a program needn't handle non-finite values.
Results may differ from a plain program's by a relative error of at most 0.00038.
Values sent between devices are 32-bit elements; how exact they have to be, the bound alone decides.
No kernel may reach another device: no remote copies, remote signals or barrier semaphores. Data moves between devices by JAX's collectives and lax.ppermute only.
A program may use at most 128 MiB of HBM per device.

v0:
```python
import jax
import jax.numpy as jnp
from jax import lax
from jax.sharding import PartitionSpec as P

PB = 128
ITERS = 3
BK = 8


cheb_low = 0.05
cheb_high = 2.0


def local(resid_deriv, local_deriv, inv_factor, block_ids, right_sides, damping):
    n_row = lax.axis_size("row")
    n_col = lax.axis_size("col")
    block_count = n_row * n_col
    capacity = BK // n_row
    bundle_count, row_count, param_width = resid_deriv.shape
    sector = block_ids[0]
    positions = jnp.arange(BK, dtype=jnp.int32)
    matches = (block_ids[:, :, None] == sector[None, None, :]).astype(jnp.int32)
    column_order = jnp.sum(matches * positions[None, :, None], axis=1)
    block_view = resid_deriv.reshape(bundle_count, row_count, BK, PB)
    arranged = jnp.take_along_axis(block_view, column_order[:, None, :, None], axis=2)
    arranged = arranged.reshape(bundle_count, row_count, param_width)
    stacked = arranged.reshape(bundle_count * row_count, param_width)
    gram_sum = lax.dot_general(
        stacked, stacked, (((0,), (0,)), ((), ())), preferred_element_type=jnp.float32
    )
    coupled = jnp.einsum("bmg,bmn->bgn", arranged, local_deriv, preferred_element_type=jnp.float32)
    projected = jnp.einsum(
        "bgn,bnk->bgk", coupled, inv_factor, precision=lax.Precision.HIGHEST
    ).astype(jnp.bfloat16)
    removed = jnp.einsum("bgk,bhk->gh", projected, projected, preferred_element_type=jnp.float32)
    region = gram_sum - removed
    region_tiles = region.reshape(BK, PB, BK, PB).transpose(0, 2, 1, 3).reshape(BK * BK, PB, PB)
    residue = sector % n_row
    groups = sector // n_row
    owner_index = (residue[:, None] * n_col + groups[None, :]).reshape(-1)
    earlier = (residue[None, :] == residue[:, None]) & (positions[None, :] < positions[:, None])
    slot_rank = jnp.sum(earlier.astype(jnp.int32), axis=1)
    owner_slot = jnp.broadcast_to(slot_rank[:, None], (BK, BK)).reshape(-1)
    local_place = (groups[:, None] * n_row + residue[None, :]).reshape(-1)
    outgoing = (
        jnp.zeros((block_count, capacity, PB, PB), jnp.float32)
        .at[owner_index, owner_slot]
        .set(region_tiles)
    )
    labels = jnp.full((block_count, capacity), float(block_count), jnp.float32)
    labels = labels.at[owner_index, owner_slot].set(local_place.astype(jnp.float32))
    arrived, arrived_labels = (
        lax.all_to_all(outgoing, ("row", "col"), split_axis=0, concat_axis=0, tiled=True),
        lax.all_to_all(labels, ("row", "col"), split_axis=0, concat_axis=0, tiled=True),
    )
    arrived = arrived.reshape(block_count * capacity, PB, PB)
    arrived_labels = arrived_labels.reshape(block_count * capacity).astype(jnp.int32)
    summed = jax.ops.segment_sum(arrived, arrived_labels, num_segments=block_count + 1)[
        :block_count
    ]
    local_block = (
        summed.reshape(n_col, n_row, PB, PB).transpose(0, 2, 1, 3).reshape(n_col, PB, n_row * PB)
    )
    row_index = lax.axis_index("row")
    col_index = lax.axis_index("col")
    corner = lax.dynamic_slice(local_block, (col_index, 0, row_index * PB), (1, PB, PB))[0]
    pivot = corner + jnp.diag(damping)
    local_block = lax.dynamic_update_slice(local_block, pivot[None], (col_index, 0, row_index * PB))
    normal = local_block[:, None]
    matrix = local_block.reshape(n_col * PB, n_row * PB)
    pivot_factor = lax.linalg.cholesky(pivot)

    def precondition(vector_in):
        forward = lax.linalg.triangular_solve(pivot_factor, vector_in, left_side=True, lower=True)
        return lax.linalg.triangular_solve(
            pivot_factor, forward, left_side=True, lower=True, transpose_a=True
        )

    center = (cheb_high + cheb_low) / 2.0
    radius = (cheb_high - cheb_low) / 2.0
    ratio = center / radius
    weight_now = 1.0 / ratio
    residual = right_sides
    update = precondition(residual) / center
    solution = jnp.zeros_like(right_sides)
    for sweep in range(ITERS):
        solution = solution + update
        if sweep + 1 < ITERS:
            partial_cols = lax.dot_general(
                matrix,
                lax.all_gather(update, "col", axis=0, tiled=True),
                (((0,), (0,)), ((), ())),
                precision=lax.Precision.HIGHEST,
            )
            residual = residual - lax.psum_scatter(
                partial_cols, "row", scatter_dimension=0, tiled=True
            )
            weight_next = 1.0 / (2.0 * ratio - weight_now)
            update = weight_next * weight_now * update + 2.0 * weight_next / radius * precondition(
                residual
            )
            weight_now = weight_next
    return (normal, solution)


def solution(mesh):
    return jax.shard_map(
        local,
        mesh=mesh,
        in_specs=(
            P(("row", "col"), None, None),
            P(("row", "col"), None, None),
            P(("row", "col"), None, None),
            P(("row", "col"), None),
            P(("col", "row"), None),
            P(("col", "row")),
        ),
        out_specs=(P(None, "row", None, "col"), P(("col", "row"), None)),
        check_vma=False,
    )
```

profile of v0, /device:TPU:0, one launch (start us, length us, event | category | flops | bytes accessed | tf_op | source)
XLA Modules:
  0.0 411.3 jit_solution(6575646375400451075)
XLA Ops:
  9.2 3.5 scatter_fusion
  13.4 7.3 %all-to-all-start = ((f32[32,1,2]{2,1,0:T(1,128)}), f32[32,1,2]{2,1,0:T(1,128)S(1)}, u32[]{:S(2)}, u32[]{:S(2)}) async-start(f32[32,1,2]{2,1,0:T(1,128)} %copy.51), calls=%async_computation | async-start | bytes 32768 | tf_op jit(solution)/shard_map/all_to_all | solution.py:55
  21.6 11.4 %copy.52 = bf16[8,512,1024]{1,2,0:T(8,128)(2,1)} copy(bf16[8,512,1024]{2,1,0:T(8,128)(2,1)} %param.10) | data formatting | bytes 16777216 | tf_op args[0]
  33.0 11.4 %copy.53 = bf16[8,512,8,128]{3,1,2,0:T(8,128)(2,1)} copy(bf16[8,512,8,128]{1,3,2,0:T(8,128)(2,1)} %bitcast.106) | data formatting | bytes 16777216 | tf_op jit(solution)/shard_map/reshape | solution.py:25
  44.4 9.2 %gather_fusion = bf16[64,512,128]{2,1,0:T(8,128)(2,1)} fusion(bf16[8,512,8,128]{3,1,2,0:T(8,128)(2,1)} %copy.53, s32[64]{0:T(128)S(1)} %reshape.279), kind=kCustom, calls=%fused_computation | custom fusion | bytes 16777728 | tf_op jit(solution)/shard_map/jit(take_along_axis)/gather | solution.py:26
  53.6 11.4 %copy.63 = bf16[8,512,8,128]{1,3,2,0:T(8,128)(2,1)} copy(bf16[8,512,8,128]{3,1,2,0:T(8,128)(2,1)} %bitcast.104) | data formatting | bytes 16777216 | tf_op jit(solution)/shard_map/jit(take_along_axis)/gather | solution.py:26
  65.2 4.7 %bitcast_select_fusion = bf16[8,512,1024]{1,2,0:T(8,128)(2,1)S(1)} fusion(bf16[8,512,8,128]{1,3,2,0:T(8,128)(2,1)} %copy.63, pred[8,1024]{1,0:T(8,128)(4,1)S(1)} %broadcast_bitcast_fusion), kind=kLoop, calls=%fused_computation.7 | loop fusion | flops 4194304 | bytes 16785408 | tf_op jit(solution)/shard_map/jit(take_along_axis)/select_n | solution.py:26
  69.9 2.3 fusion.33
  72.2 4.3 %fusion.34 = bf16[8,1024,128]{2,1,0:T(8,128)(2,1)S(1)} fusion(f32[8,1024,128]{2,1,0:T(8,128)S(1)} %fusion.33, f32[8,128,128]{2,1,0:T(8,128)S(1)} %copy-done.3), kind=kOutput, calls=%fused_computation.79 | convolution fusion | flops 1610612736 | bytes 6815744 | tf_op jit(solution)/shard_map/bgn,bnk->bgk/dot_general | solution.py:33
  76.6 4.3 %fusion.37 = f32[1024,1024,1]{1,0,2:T(8,128)} fusion(bf16[8,1024,128]{2,1,0:T(8,128)(2,1)S(1)} %fusion.34), kind=kOutput, calls=%fused_computation.82 | convolution fusion | flops 2147483648 | bytes 6291456 | tf_op jit(solution)/shard_map/bgk,bhk->gh/dot_general | solution.py:36
  80.9 12.0 %bitcast_select_fusion.1 = bf16[8,512,8,128]{3,2,1,0:T(8,128)(2,1)} fusion(bf16[8,8,512,128]{3,2,1,0:T(8,128)(2,1)} %bitcast.105, pred[8,8]{1,0:T(8,128)(4,1)S(1)} %compare_and_fusion), kind=kLoop, calls=%fused_computation.8 | loop fusion | flops 4194304 | bytes 16777280 | tf_op jit(solution)/shard_map/jit(take_along_axis)/select_n | solution.py:26
  92.9 16.9 %fusion.3 = f32[128,8,8,128]{3,1,2,0:T(8,128)S(1)} fusion(f32[1024,1024,1]{1,0,2:T(8,128)} %fusion.37, bf16[512,8,8,128]{3,2,1,0:T(8,128)(2,1)} %bitcast.113), kind=kOutput, calls=%fused_computation.10 | convolution fusion | flops 8590983168 | bytes 16777216 | tf_op jit(solution)/shard_map/dot_general | solution.py:29
  110.8 2.7 copy.57
  113.6 2.4 broadcast_in_dim.77
  116.0 12.7 %scatter_fusion.1 = f32[32,2,128,128]{3,2,1,0:T(8,128)} fusion(f32[32,2,128,128]{3,2,1,0:T(8,128)} %broadcast_in_dim.77, s32[64]{0:T(128)S(1)} %fusion.30, f32[64,128,128]{2,1,0:T(8,128)} %bitcast.111), kind=kCustom, calls=%fused_computation.2 | custom fusion | bytes 12583424 | tf_op jit(solution)/shard_map/scatter | solution.py:49
  128.7 6.0 %all-to-all-start.1 = ((f32[32,2,128,128]{3,2,1,0:T(8,128)}), f32[32,2,128,128]{3,2,1,0:T(8,128)}, u32[]{:S(2)}, u32[]{:S(2)}) async-start(f32[32,2,128,128]{3,2,1,0:T(8,128)} %scatter_fusion.1), calls=%async_computation.1 | async-start | bytes 8388608 | tf_op jit(solution)/shard_map/all_to_all | solution.py:54
  134.9 94.8 %all-to-all-done.1 = f32[32,2,128,128]{3,2,1,0:T(8,128)} async-done(((f32[32,2,128,128]{3,2,1,0:T(8,128)}), f32[32,2,128,128]{3,2,1,0:T(8,128)}, u32[]{:S(2)}, u32[]{:S(2)}) %all-to-all-start.1) | async-done | bytes 4194336 | tf_op jit(solution)/shard_map/all_to_all | solution.py:54
  230.0 9.0 %scatter_fusion.2 = f32[33,128,128]{2,1,0:T(8,128)S(1)} fusion(f32[33,128,128]{2,1,0:T(8,128)S(1)} %broadcast_in_dim.74, s32[64]{0:T(128)S(1)} %reshape.299, f32[64,128,128]{2,1,0:T(8,128)} %bitcast.14), kind=kCustom, calls=%fused_computation.3 | custom fusion | flops 1048576 | bytes 12583168 | tf_op jit(solution)/shard_map/scatter-add | solution.py:59
  239.0 1.5 slice.22
  240.5 1.9 copy.58
  242.8 11.7 %cholesky.19 = f32[128,128]{1,0:T(8,128)S(1)} custom-call(f32[128,128]{1,0:T(8,128)S(1)} %fusion.23), custom_call_target="Cholesky" | custom-call | tf_op jit(solution)/shard_map/cholesky | solution.py:72
  255.9 9.8 %custom-call.19 = f32[1,128,128]{1,2,0:T(8,128)S(1)} custom-call(f32[1,128,128]{2,1,0:T(8,128)S(1)} %fusion.13), custom_call_target="InvertDiagBlocksLowerTriangular" | custom-call | tf_op jit(solution)/shard_map/triangular_solve/custom-call.2 | solution.py:76
  267.0 1.8 copy.61
  268.8 36.3 %all-gather.3.cloned.1.call-done = f32[1024,256]{1,0:T(8,128)} async-done(((f32[128,256]{1,0:T(8,128)}), f32[1024,256]{1,0:T(8,128)}) %all-gather.3.cloned.1.call-update) | async-done | bytes 1048592 | tf_op jit(solution)/shard_map/all_gather | solution.py:92
  305.2 6.1 %fusion.35 = f32[512,256]{1,0:T(8,128)} fusion(f32[1024,512]{1,0:T(8,128)} %bitcast.109, f32[1024,256]{1,0:T(8,128)} %all-gather.3.cloned.1.call-done), kind=kOutput, calls=%fused_computation.80 | convolution fusion | flops 1610612736 | bytes 3670016 | tf_op jit(solution)/shard_map/dot_general | solution.py:90
  311.6 20.2 %reduce-scatter.3.cloned.1.call-done = f32[128,256]{1,0:T(8,128)} async-done(((f32[512,256]{1,0:T(8,128)}), f32[128,256]{1,0:T(8,128)}) %reduce-scatter.3.cloned.1.call-update) | async-done | bytes 131088 | tf_op jit(solution)/shard_map/reduce_scatter | solution.py:96
  334.1 40.8 %all-gather.5.cloned.1.call-done = f32[1024,256]{1,0:T(8,128)} async-done(((f32[128,256]{1,0:T(8,128)}), f32[1024,256]{1,0:T(8,128)}) %all-gather.5.cloned.1.call-update) | async-done | bytes 1048592 | tf_op jit(solution)/shard_map/all_gather | solution.py:92
  374.8 6.1 %fusion.36 = f32[512,256]{1,0:T(8,128)} fusion(f32[1024,512]{1,0:T(8,128)} %bitcast.110, f32[1024,256]{1,0:T(8,128)} %all-gather.5.cloned.1.call-done), kind=kOutput, calls=%fused_computation.81 | convolution fusion | flops 1610612736 | bytes 3670016 | tf_op jit(solution)/shard_map/dot_general | solution.py:90
  381.0 1.8 copy.62
  382.8 18.7 %reduce-scatter.5.cloned.1.call-done = f32[128,256]{1,0:T(8,128)} async-done(((f32[512,256]{1,0:T(8,128)}), f32[128,256]{1,0:T(8,128)}) %reduce-scatter.5.cloned.1.call-update) | async-done | bytes 131088 | tf_op jit(solution)/shard_map/reduce_scatter | solution.py:96
  401.5 1.2 fusion.11
  402.7 1.8 fusion.10
  (54 shorter events, 10.7 us)
Async XLA Ops:
  7.2 62.7 %copy-start = (bf16[8,512,128]{2,1,0:T(8,128)(2,1)S(1)}, bf16[8,512,128]{2,1,0:T(8,128)(2,1)}, u32[]{:S(2)}) copy-start(bf16[8,512,128]{2,1,0:T(8,128)(2,1)} %param.11) | copy-start | bytes 3145732
  13.4 115.3 %all-to-all-start = ((f32[32,1,2]{2,1,0:T(1,128)}), f32[32,1,2]{2,1,0:T(1,128)S(1)}, u32[]{:S(2)}, u32[]{:S(2)}) async-start(f32[32,1,2]{2,1,0:T(1,128)} %copy.51), calls=%async_computation | async-start | bytes 32768 | tf_op jit(solution)/shard_map/all_to_all | solution.py:55
  69.9 2.4 copy-start.3
  128.7 101.0 %all-to-all-start.1 = ((f32[32,2,128,128]{3,2,1,0:T(8,128)}), f32[32,2,128,128]{3,2,1,0:T(8,128)}, u32[]{:S(2)}, u32[]{:S(2)}) async-start(f32[32,2,128,128]{3,2,1,0:T(8,128)} %scatter_fusion.1), calls=%async_computation.1 | async-start | bytes 8388608 | tf_op jit(solution)/shard_map/all_to_all | solution.py:54
  134.7 170.5 %all-gather.3.cloned.1.call-start = ((), (), s32[]{:S(2)}) async-start(), calls=%async_computation.4 | async-start | bytes 1179648 | tf_op jit(solution)/shard_map/all_gather | solution.py:92
  239.0 3.4 copy-start.4
  239.0 26.7 %copy-start.2 = (f32[128,256]{1,0:T(8,128)S(1)}, f32[128,256]{1,0:T(8,128)}, u32[]{:S(2)}) copy-start(f32[128,256]{1,0:T(8,128)} %param.14) | copy-start | bytes 393220
  267.0 64.9 %reduce-scatter.3.cloned.1.call-start = ((), (), s32[]{:S(2)}) async-start(), calls=%async_computation.5 | async-start | bytes 655360 | tf_op jit(solution)/shard_map/reduce_scatter | solution.py:96
  311.3 63.6 %all-gather.5.cloned.1.call-start = ((), (), s32[]{:S(2)}) async-start(), calls=%async_computation.6 | async-start | bytes 1179648 | tf_op jit(solution)/shard_map/all_gather | solution.py:92
  334.0 70.5 %copy-start.1 = (bf16[8,512,128]{2,1,0:T(8,128)(2,1)S(1)}, bf16[8,512,128]{2,1,0:T(8,128)(2,1)}, u32[]{:S(2)}) copy-start(bf16[8,512,128]{2,1,0:T(8,128)(2,1)} %param.11) | copy-start | bytes 3145732
  334.0 67.5 %reduce-scatter.5.cloned.1.call-start = ((), (), s32[]{:S(2)}) async-start(), calls=%async_computation.7 | async-start | bytes 655360 | tf_op jit(solution)/shard_map/reduce_scatter | solution.py:96
Sparse Core Ops, SparseCore 0:
  267.1 38.0 all-gather.2
  311.4 20.3 reduce-scatter.2
  334.5 40.2 all-gather.4
  381.1 20.3 reduce-scatter.4
where the time goes:
time: 418 us; the launch traced here: 411 us
  waiting for transfers between devices  211 us (50%)
  local copies, waits for them, and re-layouts  74.6 us (18%)
  other arithmetic  52.2 us (12%)
  matrix products  45.6 us (11%)
  between operations  14.3 us (3%)
  starting transfers between devices  13.7 us (3%)
    all_to_all x1, waiting for transfers between devices, local(): lax.all_to_all(outgoing, ('row', 'col'), split_axis=0, concat_axis=0, til...  94.8 us
    all_gather x2, waiting for transfers between devices, local(): lax.all_gather(update, 'col', axis=0, tiled=True)  77.1 us
    reduce_scatter x2, waiting for transfers between devices, local(): lax.psum_scatter(partial_cols, 'row', scatter_dimension=0, tiled=True)  38.9 us
    gather x3, local copies, waits for them, and re-layouts, local(): jnp.take_along_axis(block_view, column_order[:, None, :, None], axis=2)  20.7 us
    dot_general x1, matrix products, local(): lax.dot_general(stacked, stacked, (((0,), (0,)), ((), ())), preferred_ele...  16.9 us
    select_n x2, other arithmetic, local(): jnp.take_along_axis(block_view, column_order[:, None, :, None], axis=2)  16.7 us
    unnamed x13, local copies, waits for them, and re-layouts  14.3 us
    scatter x1, local copies, waits for them, and re-layouts, local(): outgoing = jnp.zeros((block_count, capacity, PB, PB), jnp.float32).at[own...  12.7 us
  transfers between devices with their start and end apart: 6, of which 5 were waited for; matrix products, arithmetic and copies ran while one was open for 27% of the time, Pallas kernels for 0%

commit v1 on v0

v1 whole, which is shorter than its diff:
```python
import functools

import jax
import jax.numpy as jnp
from jax import lax
from jax.experimental import pallas as pl
from jax.experimental.pallas import tpu as pltpu
from jax.sharding import PartitionSpec as P


PB = 128
ITERS = 3

cheb_low = 0.05
cheb_high = 2.0
center = (cheb_high + cheb_low) / 2.0
radius = (cheb_high - cheb_low) / 2.0
ratio = center / radius

BOTH = ("row", "col")
VMEM = pl.BlockSpec(memory_space=pltpu.VMEM)
SMEM = pl.BlockSpec(memory_space=pltpu.SMEM)
ANY = pl.BlockSpec(memory_space=pl.ANY)
f32_dot = functools.partial(jnp.dot, preferred_element_type=jnp.float32)


def params(mib):
    return pltpu.CompilerParams(vmem_limit_bytes=mib << 20)


def split(x):
    high = x.astype(jnp.bfloat16)
    return high, (x - high.astype(jnp.float32)).astype(jnp.bfloat16)


def dot_split(a, b):
    (ah, al), (bh, bl) = a, b
    return f32_dot(ah, bh) + (f32_dot(ah, bl) + f32_dot(al, bh))


def chunk_list(capacity):
    chunks = [(0, 0, PB)]
    for slot in range(1, capacity):
        chunks += [(slot, 0, PB // 2), (slot, PB // 2, PB // 2)]
    return chunks


def region_kernel(n_row, n_col, chunks, ids, resid, local, factor, *refs):
    outs = refs[: len(chunks)]
    cols, rows, stage, sector, in_sem, out_sem = refs[len(chunks) :]
    bundles, blocks = ids.shape
    m = resid.shape[1]
    depth = bundles * m

    for b in range(bundles):
        for k in range(blocks):
            me = ids[b, k]
            rank = jnp.int32(0)
            for j in range(blocks):
                rank = rank + (ids[b, j] < me).astype(jnp.int32)
            pltpu.make_async_copy(
                resid.at[b, :, pl.ds(k * PB, PB)], cols.at[rank, pl.ds(b * m, m), :], in_sem.at[b]
            ).start()
            if b == 0:
                sector[rank] = me

    for b in range(bundles):
        here = cols.at[:, pl.ds(b * m, m), :]
        pltpu.make_async_copy(here, here, in_sem.at[b]).wait()
        for p in range(blocks):
            rows[p * PB : (p + 1) * PB, b * m : (b + 1) * m] = cols[p, b * m : (b + 1) * m, :].T
        coupled = f32_dot(rows[:, b * m : (b + 1) * m], local[b])
        projected = dot_split(split(coupled), split(factor[b])).astype(jnp.bfloat16)
        n = projected.shape[1]
        at = depth + b * n
        rows[:, at : at + n] = -projected
        for p in range(blocks):
            cols[p, at : at + n, :] = projected[p * PB : (p + 1) * PB].T

    def send(g, h):
        mine, other = sector[g], sector[h]
        residue = lax.rem(mine, n_row)
        rank = jnp.int32(0)
        for j in range(g):
            rank = rank + (lax.rem(sector[j], n_row) == residue).astype(jnp.int32)
        owner = residue * n_col + lax.div(other, n_row)
        if g == h:
            slot = jnp.int32(0)
        elif g < h:
            slot = rank + (lax.rem(other, n_row) == residue).astype(jnp.int32)
        else:
            slot = rank
        for out, (at_slot, first, count) in zip(outs, chunks):

            @pl.when(slot == at_slot)
            def _():
                pltpu.make_async_copy(
                    stage.at[g, h, pl.ds(first, count)], out.at[owner], out_sem
                ).start()

    for i in range(0, blocks, 2):
        for j in range(i, blocks, 2):
            right = jnp.concatenate([cols[j], cols[j + 1]], axis=1)
            total = f32_dot(rows[i * PB : (i + 2) * PB, :], right)
            for x in range(2):
                for y in range(2):
                    tile = total[x * PB : (x + 1) * PB, y * PB : (y + 1) * PB]
                    stage[i + x, j + y] = tile
                    send(i + x, j + y)
                    if i != j:
                        stage[j + y, i + x] = tile.T
                        send(j + y, i + x)
    pltpu.make_async_copy(stage, stage, out_sem).wait()


def region(ids, resid, local, factor, n_row, n_col, chunks):
    bundles, m, gp = resid.shape
    blocks, n = ids.shape[1], local.shape[2]
    depth = bundles * (m + n)
    return pl.pallas_call(
        functools.partial(region_kernel, n_row, n_col, chunks),
        out_shape=[
            jax.ShapeDtypeStruct((n_row * n_col, count, PB), jnp.float32) for _, _, count in chunks
        ],
        in_specs=[SMEM, ANY, VMEM, VMEM],
        out_specs=[ANY] * len(chunks),
        scratch_shapes=[
            pltpu.VMEM((blocks, depth, PB), jnp.bfloat16),
            pltpu.VMEM((gp, depth), jnp.bfloat16),
            pltpu.VMEM((blocks, blocks, PB, PB), jnp.float32),
            pltpu.SMEM((blocks,), jnp.int32),
            pltpu.SemaphoreType.DMA((bundles,)),
            pltpu.SemaphoreType.DMA,
        ],
        compiler_params=params(52),
        name="region",
    )(ids, resid, local, factor)


def tile_places(sectors, row_index, col_index, n_row, capacity):
    residue, group = sectors % n_row, sectors // n_row
    in_row, in_col = residue == row_index, group == col_index
    has_col = jnp.any(in_col, axis=1, keepdims=True)
    column = jnp.sum(jnp.where(in_col, sectors, 0), axis=1, keepdims=True)
    lower = sectors[:, None, :] < sectors[:, :, None]
    rank = jnp.sum((lower & in_row[:, None, :]).astype(jnp.int32), axis=2)
    same = has_col & (column % n_row == row_index)
    slot = jnp.where(in_col, 0, rank + (same & (sectors < column)).astype(jnp.int32))
    place = group * n_row + column % n_row
    found = in_row & has_col
    return [
        jnp.max(jnp.where(found & (slot == s), place, -1), axis=1) for s in range(capacity)
    ]


def add_tiles(places, arrived, total, first, count):
    @pl.loop(0, arrived.shape[0])
    def _(d):
        place = places[d]

        @pl.when(place >= 0)
        def _():
            total[place, pl.ds(first, count), :] += arrived[d]


def first_kernel(places, where, arrived, damping, total, pivot):
    total[...] = jnp.zeros_like(total)
    add_tiles(places, arrived, total, 0, PB)
    line = lax.broadcasted_iota(jnp.int32, (PB, PB), 0)
    column = lax.broadcasted_iota(jnp.int32, (PB, PB), 1)
    corner = total[where[0]] + jnp.where(line == column, damping[...], 0.0)
    total[where[0]] = corner
    pivot[...] = corner


def first_tiles(places, where, arrived, damping, tiles):
    return pl.pallas_call(
        first_kernel,
        out_shape=[
            jax.ShapeDtypeStruct((tiles, PB, PB), jnp.float32),
            jax.ShapeDtypeStruct((PB, PB), jnp.float32),
        ],
        in_specs=[SMEM, SMEM, VMEM, VMEM],
        out_specs=[VMEM, VMEM],
        compiler_params=params(12),
        name="first_tiles",
    )(places, where, arrived, damping)


def more_kernel(first, count, places, arrived, total_in, total):
    add_tiles(places, arrived, total, first, count)


def more_tiles(places, arrived, total, first, count):
    return pl.pallas_call(
        functools.partial(more_kernel, first, count),
        out_shape=jax.ShapeDtypeStruct(total.shape, jnp.float32),
        in_specs=[SMEM, VMEM, VMEM],
        out_specs=VMEM,
        input_output_aliases={2: 0},
        compiler_params=params(12),
        name="more_tiles",
    )(places, arrived, total)


def products(where, vectors, high, low, both, keep, away):
    n_row = keep.shape[0] * 2
    for mask, vector in enumerate(vectors):
        at = pl.multiple_of((where[2] ^ mask) * PB, PB)
        vh, vl = split(vector[...])
        both[0, :, pl.ds(at, PB)] = vh
        both[1, :, pl.ds(at, PB)] = vl
    result = dot_split((both[0], both[1]), (high[...], low[...]))
    for sub in range(n_row):
        mask = where[1] ^ sub
        part = result[:, sub * PB : (sub + 1) * PB]

        @pl.when(mask % 2 == 0)
        def _():
            keep[mask // 2] = part

        @pl.when(mask % 2 == 1)
        def _():
            away[mask // 2] = part


def finish_kernel(first, count, n_vec, places, where, arrived, total_in, *refs):
    vectors = refs[:n_vec]
    normal, high, low, keep, away, both, total = refs[n_vec:]
    n_row = keep.shape[0] * 2
    if count:
        total[...] = total_in[...]
        add_tiles(places, arrived, total, first, count)
    else:
        total = total_in
    for a in range(n_vec):
        for sub in range(n_row):
            tile = total[a * n_row + sub]
            normal[a, 0, :, sub * PB : (sub + 1) * PB] = tile
            th, tl = split(tile)
            high[a * PB : (a + 1) * PB, sub * PB : (sub + 1) * PB] = th
            low[a * PB : (a + 1) * PB, sub * PB : (sub + 1) * PB] = tl
    products(where, vectors, high, low, both, keep, away)


def finish(places, where, arrived, total, vectors, n_row, first, count):
    n_col = len(vectors)
    wide = vectors[0].shape[0]
    halves = jax.ShapeDtypeStruct((n_row // 2, wide, PB), jnp.float32)
    return pl.pallas_call(
        functools.partial(finish_kernel, first, count, n_col),
        out_shape=[
            jax.ShapeDtypeStruct((n_col, 1, PB, n_row * PB), jnp.float32),
            jax.ShapeDtypeStruct((n_col * PB, n_row * PB), jnp.bfloat16),
            jax.ShapeDtypeStruct((n_col * PB, n_row * PB), jnp.bfloat16),
            halves,
            halves,
        ],
        in_specs=[SMEM, SMEM, VMEM, VMEM] + [VMEM] * n_col,
        out_specs=[VMEM] * 5,
        scratch_shapes=[
            pltpu.VMEM((2, wide, n_col * PB), jnp.bfloat16),
            pltpu.VMEM(total.shape, jnp.float32),
        ],
        compiler_params=params(24),
        name="finish",
    )(places, where, arrived, total, *vectors)


def apply_kernel(n_vec, where, high, low, *refs):
    vectors = refs[:n_vec]
    keep, away, both = refs[n_vec:]
    products(where, vectors, high, low, both, keep, away)


def apply_matrix(where, high, low, vectors, n_row):
    n_col = len(vectors)
    wide = vectors[0].shape[0]
    halves = jax.ShapeDtypeStruct((n_row // 2, wide, PB), jnp.float32)
    return pl.pallas_call(
        functools.partial(apply_kernel, n_col),
        out_shape=[halves, halves],
        in_specs=[SMEM, VMEM, VMEM] + [VMEM] * n_col,
        out_specs=[VMEM] * 2,
        scratch_shapes=[pltpu.VMEM((2, wide, n_col * PB), jnp.bfloat16)],
        compiler_params=params(12),
        name="apply_matrix",
    )(where, high, low, *vectors)


def swap(x, axis, mask):
    return lax.ppermute(x, axis, [(i, i ^ mask) for i in range(lax.axis_size(axis))])


def gather_columns(own):
    half = lax.axis_size("col") // 2
    far = swap(own, "col", half)
    near = [own] + [swap(own, "col", mask) for mask in range(1, half)]
    beyond = [far] + [swap(far, "col", mask) for mask in range(1, half)]
    return near + beyond


def sum_rows(keep, away):
    mask = 1
    while True:
        summed = keep + swap(away, "row", mask)
        mask *= 2
        if mask == lax.axis_size("row"):
            return summed[0]
        keep, away = summed[0::2], summed[1::2]


def exchange(x):
    return lax.all_to_all(x, BOTH, split_axis=0, concat_axis=0, tiled=True)


def body(resid_deriv, local_deriv, inv_factor, block_ids, right_sides, damping):
    n_row, n_col = lax.axis_size("row"), lax.axis_size("col")
    devices = n_row * n_col
    capacity = max(block_ids.shape[1] // n_row, 1)
    chunks = chunk_list(capacity)
    row_index, col_index = lax.axis_index("row"), lax.axis_index("col")
    where = jnp.stack([col_index * n_row + row_index, row_index, col_index]).astype(jnp.int32)

    sends = region(block_ids, resid_deriv, local_deriv, inv_factor, n_row, n_col, chunks)
    arrived = []
    for x in sends:
        arrived.append(exchange(x))
    sectors = exchange(jnp.broadcast_to(block_ids[:1], (devices, block_ids.shape[1])))
    places = tile_places(sectors, row_index, col_index, n_row, capacity)

    total, pivot = first_tiles(places[0], where, arrived[0], damping[None, :], devices)
    factor = lax.linalg.cholesky(pivot)
    inverse_factor = lax.linalg.triangular_solve(
        factor, jnp.eye(PB, dtype=jnp.float32), left_side=True, lower=True
    )
    high_dot = functools.partial(jnp.dot, precision=lax.Precision.HIGHEST)
    inverse = high_dot(inverse_factor.T, inverse_factor)
    residual = right_sides.T
    update = high_dot(residual, inverse) / center
    vectors = gather_columns(update)

    for (slot, first, count), x in list(zip(chunks, arrived))[1:-1]:
        total = more_tiles(places[slot], x, total, first, count)
    slot, first, count = chunks[-1]
    normal, high, low, keep, away = finish(
        places[slot], where, arrived[-1], total, vectors, n_row, first, count if len(chunks) > 1 else 0
    )
    answer = update
    weight = 1.0 / ratio
    for sweep in range(1, ITERS):
        residual = residual - sum_rows(keep, away)
        weight_next = 1.0 / (2.0 * ratio - weight)
        update = weight_next * weight * update + 2.0 * weight_next / radius * high_dot(
            residual, inverse
        )
        weight = weight_next
        answer = answer + update
        if sweep + 1 < ITERS:
            vectors = gather_columns(update)
            keep, away = apply_matrix(where, high, low, vectors, n_row)
    return normal, answer.T


def solution(mesh):
    return jax.shard_map(
        body,
        mesh=mesh,
        in_specs=(
            P(BOTH, None, None),
            P(BOTH, None, None),
            P(BOTH, None, None),
            P(BOTH, None),
            P(("col", "row"), None),
            P(("col", "row")),
        ),
        out_specs=(P(None, "row", None, "col"), P(("col", "row"), None)),
        check_vma=False,
    )
```

time: 418 us -> 222 us (0.53); the launches traced: 411 us -> 221 us
  waiting for transfers between devices: 211 us -> 76.2 us
  local copies, waits for them, and re-layouts: 74.6 us -> 9.78 us
  matrix products: 45.6 us -> 2.39 us
  Pallas kernels: 0 us -> 40.6 us
  blocking collectives: 0 us -> 33.2 us
  other arithmetic: 52.2 us -> 23.2 us
  starting transfers between devices: 13.7 us -> 34.8 us
  between operations: 14.3 us -> 0.94 us
    all_gather x2 -> x0, waiting for transfers between devices: 77.1 us -> none  [local(): lax.all_gather(update, 'col', axis=0, tiled=True)]
    all_to_all x2 -> x3, waiting for transfers between devices: 94.8 us -> 49.7 us  [exchange(): return lax.all_to_all(x, BOTH, split_axis=0, concat_axis=0, tiled=True)]
    pallas_call x0 -> x5, Pallas kernels: none -> 40.6 us  [the longest x1 31.5 us: region(): pl.pallas_call(functools.partial(region_kernel, n_row, n_col, chunks), ou...]
    reduce_scatter x2 -> x0, waiting for transfers between devices: 38.9 us -> none  [local(): lax.psum_scatter(partial_cols, 'row', scatter_dimension=0, tiled=True)]
    dot_general x6 -> x4, matrix products: 40.1 us -> 2.14 us  [the longest x2 1.46 us: body(): high_dot(residual, inverse)]
    all_to_all x0 -> x1, blocking collectives: none -> 33.2 us  [exchange(): return lax.all_to_all(x, BOTH, split_axis=0, concat_axis=0, tiled=True)]
    ppermute x0 -> x18, waiting for transfers between devices: none -> 26.5 us  [swap(): lax.ppermute(x, axis, [(i, i ^ mask) for i in range(lax.axis_size(axis))])]
    ppermute x0 -> x18, starting transfers between devices: none -> 21.8 us  [swap(): lax.ppermute(x, axis, [(i, i ^ mask) for i in range(lax.axis_size(axis))])]
  transfers between devices with their start and end apart: 6 -> 21, of which waited for: 5 -> 13; matrix products, arithmetic and copies ran while one was open for 27% -> 11% of each run, Pallas kernels for 0% -> 15%
where the time goes in v1:
time: 222 us; the launch traced here: 221 us
  waiting for transfers between devices  76.2 us (34%)
  Pallas kernels  40.6 us (18%)
  starting transfers between devices  34.8 us (16%)
  blocking collectives  33.2 us (15%)
  other arithmetic  23.2 us (10%)
  local copies, waits for them, and re-layouts  9.78 us (4%)
  matrix products  2.39 us (1%)
    all_to_all x3, waiting for transfers between devices, exchange(): return lax.all_to_all(x, BOTH, split_axis=0, concat_axis=0, tiled=True)  49.7 us
    all_to_all x1, blocking collectives, exchange(): return lax.all_to_all(x, BOTH, split_axis=0, concat_axis=0, tiled=True)  33.2 us
    pallas_call x1, Pallas kernels, region(): pl.pallas_call(functools.partial(region_kernel, n_row, n_col, chunks), ou...  31.5 us
    ppermute x18, waiting for transfers between devices, swap(): lax.ppermute(x, axis, [(i, i ^ mask) for i in range(lax.axis_size(axis))])  26.5 us
    ppermute x18, starting transfers between devices, swap(): lax.ppermute(x, axis, [(i, i ^ mask) for i in range(lax.axis_size(axis))])  21.8 us
    all_to_all x3, starting transfers between devices, exchange(): return lax.all_to_all(x, BOTH, split_axis=0, concat_axis=0, tiled=True)  13 us
    another operation x3, other arithmetic, body(): factor = lax.linalg.cholesky(pivot)  12.4 us
    another operation x2, other arithmetic, body(): lax.linalg.triangular_solve(factor, jnp.eye(PB, dtype=jnp.float32), left_...  10.5 us
  transfers between devices with their start and end apart: 21, of which 13 were waited for; matrix products, arithmetic and copies ran while one was open for 11% of the time, Pallas kernels for 15%

profile of v1, /device:TPU:0, one launch (start us, length us, event | category | flops | bytes accessed | tf_op | source)
XLA Modules:
  0.0 221.1 jit_solution(11448976414937009563)
XLA Ops:
  1.9 7.3 %all-to-all-start = ((s32[32,1,8]{2,1,0:T(1,128)}), s32[32,1,8]{2,1,0:T(1,128)S(1)}, u32[]{:S(2)}, u32[]{:S(2)}) async-start(s32[32,1,8]{2,1,0:T(1,128)} %broadcast_in_dim.9), calls=%async_computation | async-start | bytes 32768 | tf_op jit(solution)/shard_map/all_to_all | solution.py:314
  11.0 31.5 %region.1 = (f32[32,128,128]{2,1,0:T(8,128)}, f32[32,64,128]{2,1,0:T(8,128)S(1)}, f32[32,64,128]{2,1,0:T(8,128)}) custom-call(s32[8,8]{1,0:T(8,128)S(1)} %copy-done.8, bf16[8,512,1024]{2,1,0:T(8,128)(2,1)} %resid.1, bf16[8,512,128]{2,1,0:T(8,128)(2,1)} %local.1, f32[8,128,128]{2,1,0:T(8,128)S(1)} %copy-done.7), custom_call_target="tpu_custom_call" | custom-call | tf_op jit(solution)/shard_map/region/pallas_call | solution.py:120
  42.5 33.2 %all_to_all.24.arrived = f32[32,64,128]{2,1,0:T(8,128)} all-to-all(f32[32,64,128]{2,1,0:T(8,128)S(1)} %get-tuple-element.15), channel_id=1, replica_groups=mesh['row'=4,'col'=8] {'row','col'}, dimensions={0} | all-to-all | bytes 2097152 | tf_op jit(solution)/shard_map/all_to_all | solution.py:314
  75.7 2.7 %all-to-all-start.3 = ((f32[32,128,128]{2,1,0:T(8,128)}), f32[32,128,128]{2,1,0:T(8,128)S(1)}, u32[]{:S(2)}, u32[]{:S(2)}) async-start(f32[32,128,128]{2,1,0:T(8,128)} %get-tuple-element.16), calls=%async_computation.3 | async-start | bytes 4194304 | tf_op jit(solution)/shard_map/all_to_all | solution.py:314
  78.7 49.7 %all-to-all-done.3.arrived = f32[32,128,128]{2,1,0:T(8,128)S(1)} async-done(((f32[32,128,128]{2,1,0:T(8,128)}), f32[32,128,128]{2,1,0:T(8,128)S(1)}, u32[]{:S(2)}, u32[]{:S(2)}) %all-to-all-start.3) | async-done | bytes 2097184 | tf_op jit(solution)/shard_map/all_to_all | solution.py:314
  128.4 2.9 %all-to-all-start.1 = ((f32[32,64,128]{2,1,0:T(8,128)}), f32[32,64,128]{2,1,0:T(8,128)S(1)}, u32[]{:S(2)}, u32[]{:S(2)}) async-start(f32[32,64,128]{2,1,0:T(8,128)} %get-tuple-element.14), calls=%async_computation.1 | async-start | bytes 2097152 | tf_op jit(solution)/shard_map/all_to_all | solution.py:314
  131.4 1.6 copy-done.1
  134.5 11.7 %cholesky.17 = f32[128,128]{1,0:T(8,128)S(1)} custom-call(f32[128,128]{1,0:T(8,128)S(1)} %fusion.10), custom_call_target="Cholesky" | custom-call | tf_op jit(solution)/shard_map/cholesky | solution.py:333
  147.5 9.8 %custom-call.5 = f32[1,128,128]{1,2,0:T(8,128)S(1)} custom-call(f32[1,128,128]{2,1,0:T(8,128)S(1)} %fusion.7), custom_call_target="InvertDiagBlocksLowerTriangular" | custom-call | tf_op jit(solution)/shard_map/triangular_solve | solution.py:334
  158.3 2.7 %collective-permute-start.3 = (f32[256,128]{1,0:T(8,128)S(1)}, f32[256,128]{1,0:T(8,128)S(1)}, u32[]{:S(2)}, u32[]{:S(2)}) collective-permute-start(f32[256,128]{1,0:T(8,128)S(1)} %multiply_bitcast_fusion.refs_0_), channel_id=1, source_target_pairs={{0,4},{1,5},{2,6},{3,7},{4,0},{5,1},{6,2},{7,3},{8,12},{9,13},{10,... | collective-permute-start | bytes 393224 | tf_op jit(solution)/shard_map/ppermute | solution.py:292
  161.1 1.5 collective-permute-start
  162.5 1.5 collective-permute-start.1
  164.6 3.3 %collective-permute-done.3.refs_4_ = f32[256,128]{1,0:T(8,128)S(1)} collective-permute-done((f32[256,128]{1,0:T(8,128)S(1)}, f32[256,128]{1,0:T(8,128)S(1)}, u32[]{:S(2)}, u32[]{:S(2)}) %collective-permute-start.3) | collective-permute-done | bytes 131104 | tf_op jit(solution)/shard_map/ppermute | solution.py:292
  167.9 1.6 collective-permute-start.4
  169.9 1.5 collective-permute-start.6
  173.6 1.8 collective-permute-done.4.refs_5_
  176.0 1.9 collective-permute-done.6.refs_7_
  177.8 4.8 %finish.1 = (f32[8,1,128,512]{3,2,1,0:T(8,128)}, bf16[1024,512]{1,0:T(8,128)(2,1)S(1)}, bf16[1024,512]{1,0:T(8,128)(2,1)S(1)}, f32[2,256,128]{2,1,0:T(8,128)S(1)}, f32[2,256,128]{2,1,0:T(8,128)S(1)}) custom-call(s32[32]{0:T(128)S(1)} %get-tuple-element.35.places, s32[3]{0:T(128)S(1)} %pad_add_fusion.where, f32[32,64,128]{2,1,0:T(8,128)S(1)} %all-to-all-done.1.arrived, ...), custom_call_target="tpu_custom_call" | custom-call | tf_op jit(solution)/shard_map/finish/pallas_call | solution.py:250
  184.6 1.5 collective-permute-done.7
  186.2 1.5 collective-permute-start.8
  188.7 3.1 %collective-permute-done.8 = f32[1,256,128]{2,1,0:T(8,128)S(1)} collective-permute-done((f32[1,256,128]{2,1,0:T(8,128)S(1)}, f32[1,256,128]{2,1,0:T(8,128)S(1)}, u32[]{:S(2)}, u32[]{:S(2)}) %collective-permute-start.8) | collective-permute-done | bytes 131104 | tf_op jit(solution)/shard_map/ppermute | solution.py:292
  193.0 1.8 collective-permute-start.12
  194.8 1.7 collective-permute-start.10
  198.3 3.2 %collective-permute-done.12.refs_4_ = f32[256,128]{1,0:T(8,128)S(1)} collective-permute-done((f32[256,128]{1,0:T(8,128)S(1)}, f32[256,128]{1,0:T(8,128)S(1)}, u32[]{:S(2)}, u32[]{:S(2)}) %collective-permute-start.12) | collective-permute-done | bytes 131104 | tf_op jit(solution)/shard_map/ppermute | solution.py:292
  201.5 1.4 collective-permute-start.13
  202.9 2.1 collective-permute-start.15
  205.7 3.1 %collective-permute-done.13.refs_5_ = f32[256,128]{1,0:T(8,128)S(1)} collective-permute-done((f32[256,128]{1,0:T(8,128)S(1)}, f32[256,128]{1,0:T(8,128)S(1)}, u32[]{:S(2)}, u32[]{:S(2)}) %collective-permute-start.13) | collective-permute-done | bytes 131104 | tf_op jit(solution)/shard_map/ppermute | solution.py:292
  208.8 2.0 collective-permute-done.15.refs_7_
  210.8 2.0 apply_matrix.1
  212.9 1.5 collective-permute-done.16
  214.5 1.7 collective-permute-start.17
  216.2 3.9 %collective-permute-done.17 = f32[1,256,128]{2,1,0:T(8,128)S(1)} collective-permute-done((f32[1,256,128]{2,1,0:T(8,128)S(1)}, f32[1,256,128]{2,1,0:T(8,128)S(1)}, u32[]{:S(2)}, u32[]{:S(2)}) %collective-permute-start.17) | collective-permute-done | bytes 131104 | tf_op jit(solution)/shard_map/ppermute | solution.py:292
  (75 shorter events, 18.5 us)
Async XLA Ops:
  1.9 40.6 %all-to-all-start = ((s32[32,1,8]{2,1,0:T(1,128)}), s32[32,1,8]{2,1,0:T(1,128)S(1)}, u32[]{:S(2)}, u32[]{:S(2)}) async-start(s32[32,1,8]{2,1,0:T(1,128)} %broadcast_in_dim.9), calls=%async_computation | async-start | bytes 32768 | tf_op jit(solution)/shard_map/all_to_all | solution.py:314
  75.7 52.7 %all-to-all-start.3 = ((f32[32,128,128]{2,1,0:T(8,128)}), f32[32,128,128]{2,1,0:T(8,128)S(1)}, u32[]{:S(2)}, u32[]{:S(2)}) async-start(f32[32,128,128]{2,1,0:T(8,128)} %get-tuple-element.16), calls=%async_computation.3 | async-start | bytes 4194304 | tf_op jit(solution)/shard_map/all_to_all | solution.py:314
  78.5 52.9 %copy-start.9 = (f32[128]{0:T(128)S(1)}, f32[128]{0:T(128)}, u32[]{:S(2)}) copy-start(f32[128]{0:T(128)} %param.11) | copy-start | bytes 1540
  128.4 3.0 %copy-start = (f32[32,128,128]{2,1,0:T(8,128)}, f32[32,128,128]{2,1,0:T(8,128)S(1)}, u32[]{:S(2)}) copy-start(f32[32,128,128]{2,1,0:T(8,128)S(1)} %all-to-all-done.3.arrived) | copy-start | bytes 6291460
  128.4 29.4 %copy-start.14 = (f32[128,256]{1,0:T(8,128)S(1)}, f32[128,256]{1,0:T(8,128)}, u32[]{:S(2)}) copy-start(f32[128,256]{1,0:T(8,128)} %param.10) | copy-start | bytes 393220
  128.4 45.2 %all-to-all-start.1 = ((f32[32,64,128]{2,1,0:T(8,128)}), f32[32,64,128]{2,1,0:T(8,128)S(1)}, u32[]{:S(2)}, u32[]{:S(2)}) async-start(f32[32,64,128]{2,1,0:T(8,128)} %get-tuple-element.14), calls=%async_computation.1 | async-start | bytes 2097152 | tf_op jit(solution)/shard_map/all_to_all | solution.py:314
  131.4 1.6 copy-start.1
  157.9 13.5 %copy-start.12 = (f32[128,128]{1,0:T(8,128)}, f32[128,128]{1,0:T(8,128)S(1)}, u32[]{:S(2)}) copy-start(f32[128,128]{1,0:T(8,128)S(1)} %fusion.22) | copy-start | bytes 196612
  158.3 13.1 %copy-start.10 = (f32[128,256]{0,1:T(8,128)}, f32[128,256]{0,1:T(8,128)S(1)}, u32[]{:S(2)}) copy-start(f32[128,256]{0,1:T(8,128)S(1)} %fusion.23) | copy-start | bytes 393220
  158.3 9.5 %collective-permute-start.3 = (f32[256,128]{1,0:T(8,128)S(1)}, f32[256,128]{1,0:T(8,128)S(1)}, u32[]{:S(2)}, u32[]{:S(2)}) collective-permute-start(f32[256,128]{1,0:T(8,128)S(1)} %multiply_bitcast_fusion.refs_0_), channel_id=1, source_target_pairs={{0,4},{1,5},{2,6},{3,7},{4,0},{5,1},{6,2},{7,3},{8,12},{9,13},{10,... | collective-permute-start | bytes 393224 | tf_op jit(solution)/shard_map/ppermute | solution.py:292
  161.1 8.8 %collective-permute-start = (f32[256,128]{1,0:T(8,128)S(1)}, f32[256,128]{1,0:T(8,128)S(1)}, u32[]{:S(2)}, u32[]{:S(2)}) collective-permute-start(f32[256,128]{1,0:T(8,128)S(1)} %multiply_bitcast_fusion.refs_0_), channel_id=1, source_target_pairs={{0,1},{1,0},{2,3},{3,2},{4,5},{5,4},{6,7},{7,6},{8,9},{9,8},{10,11... | collective-permute-start | bytes 393224 | tf_op jit(solution)/shard_map/ppermute | solution.py:292
  162.5 11.1 %collective-permute-start.1 = (f32[256,128]{1,0:T(8,128)S(1)}, f32[256,128]{1,0:T(8,128)}, u32[]{:S(2)}, u32[]{:S(2)}) collective-permute-start(f32[256,128]{1,0:T(8,128)S(1)} %multiply_bitcast_fusion.refs_0_), channel_id=1, source_target_pairs={{0,2},{1,3},{2,0},{3,1},{4,6},{5,7},{6,4},{7,5},{8,10},{9,11},{10,... | collective-permute-start | bytes 393224 | tf_op jit(solution)/shard_map/ppermute | solution.py:292
  164.1 9.6 %collective-permute-start.2 = (f32[256,128]{1,0:T(8,128)S(1)}, f32[256,128]{1,0:T(8,128)}, u32[]{:S(2)}, u32[]{:S(2)}) collective-permute-start(f32[256,128]{1,0:T(8,128)S(1)} %multiply_bitcast_fusion.refs_0_), channel_id=1, source_target_pairs={{0,3},{1,2},{2,1},{3,0},{4,7},{5,6},{6,5},{7,4},{8,11},{9,10},{10,... | collective-permute-start | bytes 393224 | tf_op jit(solution)/shard_map/ppermute | solution.py:292
  167.9 7.6 %collective-permute-start.4 = (f32[256,128]{1,0:T(8,128)S(1)}, f32[256,128]{1,0:T(8,128)}, u32[]{:S(2)}, u32[]{:S(2)}) collective-permute-start(f32[256,128]{1,0:T(8,128)S(1)} %collective-permute-done.3.refs_4_), channel_id=1, source_target_pairs={{0,1},{1,0},{2,3},{3,2},{4,5},{5,4},{6,7},{7,6},{8,9},{9,8},{10,11... | collective-permute-start | bytes 393224 | tf_op jit(solution)/shard_map/ppermute | solution.py:292
  169.5 6.5 %collective-permute-start.5 = (f32[256,128]{1,0:T(8,128)S(1)}, f32[256,128]{1,0:T(8,128)}, u32[]{:S(2)}, u32[]{:S(2)}) collective-permute-start(f32[256,128]{1,0:T(8,128)S(1)} %collective-permute-done.3.refs_4_), channel_id=1, source_target_pairs={{0,2},{1,3},{2,0},{3,1},{4,6},{5,7},{6,4},{7,5},{8,10},{9,11},{10,... | collective-permute-start | bytes 393224 | tf_op jit(solution)/shard_map/ppermute | solution.py:292
  169.9 7.9 %collective-permute-start.6 = (f32[256,128]{1,0:T(8,128)S(1)}, f32[256,128]{1,0:T(8,128)}, u32[]{:S(2)}, u32[]{:S(2)}) collective-permute-start(f32[256,128]{1,0:T(8,128)S(1)} %collective-permute-done.3.refs_4_), channel_id=1, source_target_pairs={{0,3},{1,2},{2,1},{3,0},{4,7},{5,6},{6,5},{7,4},{8,11},{9,10},{10,... | collective-permute-start | bytes 393224 | tf_op jit(solution)/shard_map/ppermute | solution.py:292
  171.3 1.2 copy-start.2
  184.6 26.2 %copy-start.4 = (bf16[1024,512]{1,0:T(8,128)(2,1)S(1)}, bf16[1024,512]{1,0:T(8,128)(2,1)}, u32[]{:S(2)}) copy-start(bf16[1024,512]{1,0:T(8,128)(2,1)} %copy-done.3) | copy-start | bytes 3145732
  184.6 26.2 %copy-start.6 = (bf16[1024,512]{1,0:T(8,128)(2,1)S(1)}, bf16[1024,512]{1,0:T(8,128)(2,1)}, u32[]{:S(2)}) copy-start(bf16[1024,512]{1,0:T(8,128)(2,1)} %copy-done.5) | copy-start | bytes 3145732
  184.6 1.5 collective-permute-start.7
  186.2 5.6 %collective-permute-start.8 = (f32[1,256,128]{2,1,0:T(8,128)S(1)}, f32[1,256,128]{2,1,0:T(8,128)S(1)}, u32[]{:S(2)}, u32[]{:S(2)}) collective-permute-start(f32[1,256,128]{2,1,0:T(8,128)S(1)} %slice.36), channel_id=1, source_target_pairs={{0,16},{8,24},{16,0},{24,8},{1,17},{9,25},{17,1},{25,9},{2,18},{10... | collective-permute-start | bytes 393224 | tf_op jit(solution)/shard_map/ppermute | solution.py:292
  193.0 8.5 %collective-permute-start.12 = (f32[256,128]{1,0:T(8,128)S(1)}, f32[256,128]{1,0:T(8,128)S(1)}, u32[]{:S(2)}, u32[]{:S(2)}) collective-permute-start(f32[256,128]{1,0:T(8,128)S(1)} %get-tuple-element.40.refs_0_), channel_id=1, source_target_pairs={{0,4},{1,5},{2,6},{3,7},{4,0},{5,1},{6,2},{7,3},{8,12},{9,13},{10,... | collective-permute-start | bytes 393224 | tf_op jit(solution)/shard_map/ppermute | solution.py:292
  194.8 8.0 %collective-permute-start.10 = (f32[256,128]{1,0:T(8,128)S(1)}, f32[256,128]{1,0:T(8,128)S(1)}, u32[]{:S(2)}, u32[]{:S(2)}) collective-permute-start(f32[256,128]{1,0:T(8,128)S(1)} %get-tuple-element.40.refs_0_), channel_id=1, source_target_pairs={{0,2},{1,3},{2,0},{3,1},{4,6},{5,7},{6,4},{7,5},{8,10},{9,11},{10,... | collective-permute-start | bytes 393224 | tf_op jit(solution)/shard_map/ppermute | solution.py:292
  196.6 9.1 %collective-permute-start.11 = (f32[256,128]{1,0:T(8,128)S(1)}, f32[256,128]{1,0:T(8,128)S(1)}, u32[]{:S(2)}, u32[]{:S(2)}) collective-permute-start(f32[256,128]{1,0:T(8,128)S(1)} %get-tuple-element.40.refs_0_), channel_id=1, source_target_pairs={{0,3},{1,2},{2,1},{3,0},{4,7},{5,6},{6,5},{7,4},{8,11},{9,10},{10,... | collective-permute-start | bytes 393224 | tf_op jit(solution)/shard_map/ppermute | solution.py:292
  197.8 7.9 %collective-permute-start.9 = (f32[256,128]{1,0:T(8,128)S(1)}, f32[256,128]{1,0:T(8,128)S(1)}, u32[]{:S(2)}, u32[]{:S(2)}) collective-permute-start(f32[256,128]{1,0:T(8,128)S(1)} %get-tuple-element.40.refs_0_), channel_id=1, source_target_pairs={{0,1},{1,0},{2,3},{3,2},{4,5},{5,4},{6,7},{7,6},{8,9},{9,8},{10,11... | collective-permute-start | bytes 393224 | tf_op jit(solution)/shard_map/ppermute | solution.py:292
  201.5 7.3 %collective-permute-start.13 = (f32[256,128]{1,0:T(8,128)S(1)}, f32[256,128]{1,0:T(8,128)S(1)}, u32[]{:S(2)}, u32[]{:S(2)}) collective-permute-start(f32[256,128]{1,0:T(8,128)S(1)} %collective-permute-done.12.refs_4_), channel_id=1, source_target_pairs={{0,1},{1,0},{2,3},{3,2},{4,5},{5,4},{6,7},{7,6},{8,9},{9,8},{10,11... | collective-permute-start | bytes 393224 | tf_op jit(solution)/shard_map/ppermute | solution.py:292
  202.9 6.0 %collective-permute-start.14 = (f32[256,128]{1,0:T(8,128)S(1)}, f32[256,128]{1,0:T(8,128)S(1)}, u32[]{:S(2)}, u32[]{:S(2)}) collective-permute-start(f32[256,128]{1,0:T(8,128)S(1)} %collective-permute-done.12.refs_4_), channel_id=1, source_target_pairs={{0,2},{1,3},{2,0},{3,1},{4,6},{5,7},{6,4},{7,5},{8,10},{9,11},{10,... | collective-permute-start | bytes 393224 | tf_op jit(solution)/shard_map/ppermute | solution.py:292
  202.9 8.0 %collective-permute-start.15 = (f32[256,128]{1,0:T(8,128)S(1)}, f32[256,128]{1,0:T(8,128)S(1)}, u32[]{:S(2)}, u32[]{:S(2)}) collective-permute-start(f32[256,128]{1,0:T(8,128)S(1)} %collective-permute-done.12.refs_4_), channel_id=1, source_target_pairs={{0,3},{1,2},{2,1},{3,0},{4,7},{5,6},{6,5},{7,4},{8,11},{9,10},{10,... | collective-permute-start | bytes 393224 | tf_op jit(solution)/shard_map/ppermute | solution.py:292
  210.8 9.2 %copy-start.11 = (f32[128,256]{0,1:T(8,128)S(1)}, f32[128,256]{0,1:T(8,128)}, u32[]{:S(2)}) copy-start(f32[128,256]{0,1:T(8,128)} %copy-done.10) | copy-start | bytes 393220
  210.8 9.2 %copy-start.13 = (f32[128,128]{1,0:T(8,128)S(1)}, f32[128,128]{1,0:T(8,128)}, u32[]{:S(2)}) copy-start(f32[128,128]{1,0:T(8,128)} %copy-done.12) | copy-start | bytes 196612
  212.8 1.6 collective-permute-start.16
  214.5 5.6 %collective-permute-start.17 = (f32[1,256,128]{2,1,0:T(8,128)S(1)}, f32[1,256,128]{2,1,0:T(8,128)S(1)}, u32[]{:S(2)}, u32[]{:S(2)}) collective-permute-start(f32[1,256,128]{2,1,0:T(8,128)S(1)} %slice.38), channel_id=1, source_target_pairs={{0,16},{8,24},{16,0},{24,8},{1,17},{9,25},{17,1},{25,9},{2,18},{10... | collective-permute-start | bytes 393224 | tf_op jit(solution)/shard_map/ppermute | solution.py:292
  (4 other events, 3.7 us)

commit v2 on v1

v2 whole, which is shorter than its diff:
```python
import functools

import jax
import jax.numpy as jnp
from jax import lax
from jax.experimental import pallas as pl
from jax.experimental.pallas import tpu as pltpu
from jax.sharding import PartitionSpec as P


PB = 128
ITERS = 3

cheb_low = 0.05
cheb_high = 2.0
center = (cheb_high + cheb_low) / 2.0
radius = (cheb_high - cheb_low) / 2.0
ratio = center / radius

BOTH = ("row", "col")
VMEM = pl.BlockSpec(memory_space=pltpu.VMEM)
SMEM = pl.BlockSpec(memory_space=pltpu.SMEM)
ANY = pl.BlockSpec(memory_space=pl.ANY)
HBM = pl.BlockSpec(memory_space=pltpu.HBM)
f32_dot = functools.partial(jnp.dot, preferred_element_type=jnp.float32)


def params(mib):
    return pltpu.CompilerParams(vmem_limit_bytes=mib << 20)


def split(x):
    high = x.astype(jnp.bfloat16)
    return high, (x - high.astype(jnp.float32)).astype(jnp.bfloat16)


def dot_split(a, b):
    (ah, al), (bh, bl) = a, b
    return f32_dot(ah, bh) + (f32_dot(ah, bl) + f32_dot(al, bh))


def chunk_list(capacity):
    chunks = [(0, 0, PB + 8)]
    for slot in range(1, capacity):
        chunks += [(slot, 0, PB // 2), (slot, PB // 2, PB // 2)]
    return chunks


def region_kernel(n_row, n_col, chunks, ids_in, resid, local_in, factor_in, *refs):
    outs = refs[: len(chunks)]
    bundles, _, gp = resid.shape
    blocks, n = gp // PB, factor_in.shape[2]
    refs = refs[len(chunks) :]
    cols, rows, coupled = refs[:bundles], refs[bundles : 2 * bundles], refs[2 * bundles :][:2]
    ids, raw, down, across, local, factor, stage, sector, in_sem, small_sem, out_sem = refs[
        2 * bundles + 2 :
    ]

    fetch_ids = pltpu.make_async_copy(ids_in, ids, small_sem.at[0])
    fetch_local = pltpu.make_async_copy(local_in, local, small_sem.at[1])
    fetch_factor = pltpu.make_async_copy(factor_in, factor, small_sem.at[2])
    fetch_ids.start()
    fetch_local.start()
    fetch_factor.start()
    fetches = [
        pltpu.make_async_copy(resid.at[b], raw.at[b], in_sem.at[b]) for b in range(bundles)
    ]
    for fetch in fetches:
        fetch.start()
    stage[0, :, PB:, :] = jnp.full((n_row * n_col, 8, PB), -1.0, jnp.float32)
    fetch_ids.wait()
    fetch_local.wait()
    fetch_factor.wait()

    def arrange(b):
        fetches[b].wait()
        for k in range(blocks):
            rank = jnp.int32(0)
            for j in range(blocks):
                if j != k:
                    rank = rank + (ids[b, j] < ids[b, k]).astype(jnp.int32)
            if b == 0:
                sector[rank] = ids[b, k]
            block = raw[b, :, k * PB : (k + 1) * PB]
            cols[b][rank] = block
            rows[b][pl.ds(pl.multiple_of(rank * PB, PB), PB), :] = block.T

    def couple(b):
        coupled[b % 2][...] = f32_dot(rows[b][...], local[b])

    def project(b):
        ch, cl = split(coupled[b % 2][...])
        fh, fl = split(factor[b])
        terms = jnp.concatenate([fh, fl], axis=1)
        parts = f32_dot(jnp.concatenate([ch, cl], axis=1), jnp.concatenate([terms, terms], axis=0))
        projected = (parts[:, :n] + parts[:, n:]).astype(jnp.bfloat16)
        across[:, b * n : (b + 1) * n] = -projected
        for p in range(blocks):
            down[p, b * n : (b + 1) * n, :] = projected[p * PB : (p + 1) * PB].T

    for step in range(bundles + 2):
        if step >= 2:
            project(step - 2)
        if 1 <= step <= bundles:
            couple(step - 1)
        if step < bundles:
            arrange(step)

    def left(i):
        parts = [r[i * PB : (i + 2) * PB, :] for r in rows] + [across[i * PB : (i + 2) * PB, :]]
        return jnp.concatenate(parts, axis=1)

    def right(j):
        pair = [[c[j + x] for c in cols] + [down[j + x]] for x in range(2)]
        return jnp.concatenate([jnp.concatenate(x, axis=0) for x in pair], axis=1)

    def put(g, h, tile):
        mine, other = sector[g], sector[h]
        residue = lax.rem(mine, n_row)
        slot = jnp.int32(0)
        if g != h:
            for j in range(g):
                slot = slot + (lax.rem(sector[j], n_row) == residue).astype(jnp.int32)
        if g < h:
            slot = slot + (lax.rem(other, n_row) == residue).astype(jnp.int32)
        owner = residue * n_col + lax.div(other, n_row)
        stage[slot, owner, :PB, :] = tile
        place = mine - residue + lax.rem(other, n_row)
        stage[0, owner, pl.ds(PB + slot, 1), :] = jnp.full((1, PB), place.astype(jnp.float32))

    for i in range(0, blocks, 2):
        for j in range(i, blocks, 2):
            total = f32_dot(left(i), right(j))
            for x in range(2):
                for y in range(2):
                    tile = total[x * PB : (x + 1) * PB, y * PB : (y + 1) * PB]
                    put(i + x, j + y, tile)
                    if i != j:
                        put(j + y, i + x, tile.T)
    copies = [
        pltpu.make_async_copy(stage.at[slot, :, pl.ds(first, count), :], out, out_sem.at[i])
        for i, (out, (slot, first, count)) in enumerate(zip(outs, chunks))
    ]
    for copy in copies:
        copy.start()
    for copy in copies:
        copy.wait()


def region(ids, resid, local, factor, n_row, n_col, capacity, chunks):
    bundles, m, gp = resid.shape
    blocks, n = ids.shape[1], local.shape[2]
    return pl.pallas_call(
        functools.partial(region_kernel, n_row, n_col, chunks),
        out_shape=[
            jax.ShapeDtypeStruct((n_row * n_col, count, PB), jnp.float32) for _, _, count in chunks
        ],
        in_specs=[HBM] * 4,
        out_specs=[HBM] * len(chunks),
        scratch_shapes=[pltpu.VMEM((blocks, m, PB), jnp.bfloat16)] * bundles
        + [pltpu.VMEM((gp, m), jnp.bfloat16)] * bundles
        + [pltpu.VMEM((gp, n), jnp.float32)] * 2
        + [
            pltpu.SMEM(ids.shape, jnp.int32),
            pltpu.VMEM(resid.shape, resid.dtype),
            pltpu.VMEM((blocks, bundles * n, PB), jnp.bfloat16),
            pltpu.VMEM((gp, bundles * n), jnp.bfloat16),
            pltpu.VMEM(local.shape, local.dtype),
            pltpu.VMEM(factor.shape, factor.dtype),
            pltpu.VMEM((capacity, n_row * n_col, PB + 8, PB), jnp.float32),
            pltpu.SMEM((blocks,), jnp.int32),
            pltpu.SemaphoreType.DMA((bundles,)),
            pltpu.SemaphoreType.DMA((3,)),
            pltpu.SemaphoreType.DMA((len(chunks),)),
        ],
        compiler_params=params(48),
        name="region",
    )(ids, resid, local, factor)


def add_tiles(places, slot, arrived, total, first, count):
    def step(d, carry):
        place = places[d, slot]

        @pl.when(place >= 0)
        def _():
            total[place, pl.ds(first, count), :] += arrived[d, :count, :]

        return carry

    lax.fori_loop(0, arrived.shape[0], step, 0)


def first_kernel(where, places, arrived, damping, total, pivot, held, sem):
    fetch = pltpu.make_async_copy(arrived, held, sem)
    fetch.start()
    total[...] = jnp.zeros_like(total)
    fetch.wait()
    add_tiles(places, 0, held, total, 0, PB)
    line = lax.broadcasted_iota(jnp.int32, (PB, PB), 0)
    column = lax.broadcasted_iota(jnp.int32, (PB, PB), 1)
    corner = total[where[0]] + jnp.where(line == column, damping[...], 0.0)
    total[where[0]] = corner
    pivot[...] = corner


def first_tiles(where, places, arrived, damping, tiles):
    return pl.pallas_call(
        first_kernel,
        out_shape=[
            jax.ShapeDtypeStruct((tiles, PB, PB), jnp.float32),
            jax.ShapeDtypeStruct((PB, PB), jnp.float32),
        ],
        in_specs=[SMEM, SMEM, ANY, VMEM],
        out_specs=[VMEM, VMEM],
        scratch_shapes=[pltpu.VMEM(arrived.shape, jnp.float32), pltpu.SemaphoreType.DMA],
        compiler_params=params(24),
        name="first_tiles",
    )(where, places, arrived, damping)


def invert_kernel(factor, rhs, inverse, turned, update):
    line = lax.broadcasted_iota(jnp.int32, (PB, PB), 0)
    column = lax.broadcasted_iota(jnp.int32, (PB, PB), 1)

    def product(a, b):
        return dot_split(split(a), split(b))

    c = jnp.where(line >= column, factor[...], 0.0)
    diagonal = jnp.sum(jnp.where(line == column, c, 0.0), axis=1, keepdims=True)
    scale = 1.0 / diagonal
    unit = c * scale
    eye = jnp.where(line == column, 1.0, 0.0)
    size = 4
    near = jnp.where((line // size == column // size) & (line > column), unit, 0.0)
    second = product(near, near)
    grown = (eye - near) + product(eye - near, second)
    while size < PB:
        size *= 2
        link = jnp.where(
            (line // size == column // size) & (line // (size // 2) != column // (size // 2)), unit, 0.0
        )
        grown = grown - product(product(grown, link), grown)
    across = jnp.sum(jnp.where(line == column, c, 0.0), axis=0, keepdims=True)
    lower = grown * (1.0 / across)
    full = product(lower.T, lower)
    inverse[...] = full
    back = rhs[...].T
    turned[...] = back
    update[...] = product(back, full) / center


def invert(factor, rhs):
    wide = rhs.shape[1]
    return pl.pallas_call(
        invert_kernel,
        out_shape=[
            jax.ShapeDtypeStruct((PB, PB), jnp.float32),
            jax.ShapeDtypeStruct((wide, PB), jnp.float32),
            jax.ShapeDtypeStruct((wide, PB), jnp.float32),
        ],
        in_specs=[VMEM, VMEM],
        out_specs=[VMEM] * 3,
        compiler_params=params(8),
        name="invert",
    )(factor, rhs)


def more_kernel(slot, first, count, places, arrived, total_in, total, held, sem):
    fetch = pltpu.make_async_copy(arrived, held, sem)
    fetch.start()
    fetch.wait()
    add_tiles(places, slot, held, total, first, count)


def more_tiles(places, arrived, total, slot, first, count):
    return pl.pallas_call(
        functools.partial(more_kernel, slot, first, count),
        out_shape=jax.ShapeDtypeStruct(total.shape, jnp.float32),
        in_specs=[SMEM, ANY, VMEM],
        out_specs=VMEM,
        input_output_aliases={2: 0},
        scratch_shapes=[pltpu.VMEM(arrived.shape, jnp.float32), pltpu.SemaphoreType.DMA],
        compiler_params=params(12),
        name="more_tiles",
    )(places, arrived, total)


def products(where, fetches, vectors, high, low, both, keep, away):
    n_row = keep.shape[0] * 2
    for mask, fetch in enumerate(fetches):
        fetch.wait()
        at = pl.multiple_of((where[2] ^ mask) * PB, PB)
        vh, vl = split(vectors[mask])
        both[0, :, pl.ds(at, PB)] = vh
        both[1, :, pl.ds(at, PB)] = vl
    result = dot_split((both[0], both[1]), (high[...], low[...]))
    for sub in range(n_row):
        mask = where[1] ^ sub
        part = result[:, sub * PB : (sub + 1) * PB]

        @pl.when(mask % 2 == 0)
        def _():
            keep[mask // 2] = part

        @pl.when(mask % 2 == 1)
        def _():
            away[mask // 2] = part


def fetch_all(sources, held, sem):
    fetches = [pltpu.make_async_copy(x, held.at[i], sem.at[i]) for i, x in enumerate(sources)]
    for fetch in fetches:
        fetch.start()
    return fetches


def finish_kernel(slot, first, count, n_vec, where, places, arrived, total_in, *refs):
    vectors = refs[:n_vec]
    normal, high, low, keep, away, total, held, gathered, both, whole, in_sem, vec_sem, out_sem = (
        refs[n_vec:]
    )
    n_row = keep.shape[0] * 2
    fetches = fetch_all(vectors, gathered, vec_sem)
    if count:
        fetch = pltpu.make_async_copy(arrived, held, in_sem)
        fetch.start()
        fetch.wait()
        add_tiles(places, slot, held, total, first, count)
    stores = []
    for a in range(n_vec):
        for sub in range(n_row):
            tile = total[a * n_row + sub]
            whole[a, :, sub * PB : (sub + 1) * PB] = tile
            th, tl = split(tile)
            high[a * PB : (a + 1) * PB, sub * PB : (sub + 1) * PB] = th
            low[a * PB : (a + 1) * PB, sub * PB : (sub + 1) * PB] = tl
        stores.append(pltpu.make_async_copy(whole.at[a], normal.at[a, 0], out_sem.at[a]))
        stores[-1].start()
    products(where, fetches, gathered, high, low, both, keep, away)
    for store in stores:
        store.wait()


def finish(where, places, arrived, total, vectors, n_row, slot, first, count):
    n_col = len(vectors)
    wide = vectors[0].shape[0]
    halves = jax.ShapeDtypeStruct((n_row // 2, wide, PB), jnp.float32)
    half = jax.ShapeDtypeStruct((n_col * PB, n_row * PB), jnp.bfloat16)
    return pl.pallas_call(
        functools.partial(finish_kernel, slot, first, count, n_col),
        out_shape=[
            jax.ShapeDtypeStruct((n_col, 1, PB, n_row * PB), jnp.float32),
            half,
            half,
            halves,
            halves,
            jax.ShapeDtypeStruct(total.shape, jnp.float32),
        ],
        in_specs=[SMEM, SMEM, ANY, VMEM] + [ANY] * n_col,
        out_specs=[ANY] + [VMEM] * 5,
        input_output_aliases={3: 5},
        scratch_shapes=[
            pltpu.VMEM(arrived.shape if count else (8, PB), jnp.float32),
            pltpu.VMEM((n_col, wide, PB), jnp.float32),
            pltpu.VMEM((2, wide, n_col * PB), jnp.bfloat16),
            pltpu.VMEM((n_col, PB, n_row * PB), jnp.float32),
            pltpu.SemaphoreType.DMA,
            pltpu.SemaphoreType.DMA((n_col,)),
            pltpu.SemaphoreType.DMA((n_col,)),
        ],
        compiler_params=params(32),
        name="finish",
    )(where, places, arrived, total, *vectors)


def apply_kernel(n_vec, where, high, low, *refs):
    vectors = refs[:n_vec]
    keep, away, gathered, both, vec_sem = refs[n_vec:]
    fetches = fetch_all(vectors, gathered, vec_sem)
    products(where, fetches, gathered, high, low, both, keep, away)


def apply_matrix(where, high, low, vectors, n_row):
    n_col = len(vectors)
    wide = vectors[0].shape[0]
    halves = jax.ShapeDtypeStruct((n_row // 2, wide, PB), jnp.float32)
    return pl.pallas_call(
        functools.partial(apply_kernel, n_col),
        out_shape=[halves, halves],
        in_specs=[SMEM, VMEM, VMEM] + [ANY] * n_col,
        out_specs=[VMEM] * 2,
        scratch_shapes=[
            pltpu.VMEM((n_col, wide, PB), jnp.float32),
            pltpu.VMEM((2, wide, n_col * PB), jnp.bfloat16),
            pltpu.SemaphoreType.DMA((n_col,)),
        ],
        compiler_params=params(12),
        name="apply_matrix",
    )(where, high, low, *vectors)


def swap(x, axis, mask):
    return lax.ppermute(x, axis, [(i, i ^ mask) for i in range(lax.axis_size(axis))])


def gather_columns(own):
    half = lax.axis_size("col") // 2
    far = swap(own, "col", half)
    near = [own] + [swap(own, "col", mask) for mask in range(1, half)]
    beyond = [far] + [swap(far, "col", mask) for mask in range(1, half)]
    return near + beyond


def sum_rows(keep, away):
    mask = 1
    while True:
        summed = keep + swap(away, "row", mask)
        mask *= 2
        if mask == lax.axis_size("row"):
            return summed[0]
        keep, away = summed[0::2], summed[1::2]


def exchange(x):
    return lax.all_to_all(x, BOTH, split_axis=0, concat_axis=0, tiled=True)


def body(resid_deriv, local_deriv, inv_factor, block_ids, right_sides, damping):
    n_row, n_col = lax.axis_size("row"), lax.axis_size("col")
    devices = n_row * n_col
    capacity = max(block_ids.shape[1] // n_row, 1)
    chunks = chunk_list(capacity)
    row_index, col_index = lax.axis_index("row"), lax.axis_index("col")
    where = jnp.stack([col_index * n_row + row_index, row_index, col_index]).astype(jnp.int32)

    sends = region(
        block_ids, resid_deriv, local_deriv, inv_factor, n_row, n_col, capacity, chunks
    )
    arrived = []
    for x in sends:
        arrived.append(exchange(x))
    places = arrived[0][:, PB : PB + capacity, 0].astype(jnp.int32)

    total, pivot = first_tiles(where, places, arrived[0], damping[None, :], devices)
    factor = lax.linalg.cholesky(pivot, symmetrize_input=False)
    inverse, residual, update = invert(factor, right_sides)
    vectors = gather_columns(update)

    for (slot, first, count), x in list(zip(chunks, arrived))[1:-1]:
        total = more_tiles(places, x, total, slot, first, count)
    slot, first, count = chunks[-1]
    normal, high, low, keep, away, _ = finish(
        where, places, arrived[-1], total, vectors, n_row, slot, first, count if slot else 0
    )
    high_dot = functools.partial(jnp.dot, precision=lax.Precision.HIGHEST)
    answer = update
    weight = 1.0 / ratio
    for sweep in range(1, ITERS):
        residual = residual - sum_rows(keep, away)
        weight_next = 1.0 / (2.0 * ratio - weight)
        update = weight_next * weight * update + 2.0 * weight_next / radius * high_dot(
            residual, inverse
        )
        weight = weight_next
        answer = answer + update
        if sweep + 1 < ITERS:
            vectors = gather_columns(update)
            keep, away = apply_matrix(where, high, low, vectors, n_row)
    return normal, answer.T


def solution(mesh):
    return jax.shard_map(
        body,
        mesh=mesh,
        in_specs=(
            P(BOTH, None, None),
            P(BOTH, None, None),
            P(BOTH, None, None),
            P(BOTH, None),
            P(("col", "row"), None),
            P(("col", "row")),
        ),
        out_specs=(P(None, "row", None, "col"), P(("col", "row"), None)),
        check_vma=False,
    )
```

time: 222 us -> 198 us (0.89)
  blocking collectives: 33.2 us -> 89.7 us
  waiting for transfers between devices: 76.2 us -> 27.4 us
  starting transfers between devices: 34.8 us -> 23 us
  other arithmetic: 23.2 us -> 13.3 us
  Pallas kernels: 40.6 us -> 31.9 us
    all_to_all x1 -> x2, blocking collectives: 33.2 us -> 89.7 us  [exchange(): return lax.all_to_all(x, BOTH, split_axis=0, concat_axis=0, tiled=True)]
    all_to_all x3 -> x1, waiting for transfers between devices: 49.7 us -> 0.01 us  [exchange(): return lax.all_to_all(x, BOTH, split_axis=0, concat_axis=0, tiled=True)]
    pallas_call x1, Pallas kernels: 31.5 us -> 17.8 us  [region(): pl.pallas_call(functools.partial(region_kernel, n_row, n_col, chunks), ou...]
    another operation x5 -> x3, other arithmetic: 22.9 us -> 12.5 us  [body(): factor = lax.linalg.cholesky(pivot, symmetrize_input=False)]
    all_to_all x3 -> x1, starting transfers between devices: 13 us -> 2.78 us  [exchange(): return lax.all_to_all(x, BOTH, split_axis=0, concat_axis=0, tiled=True)]
    pallas_call x2 -> x3, Pallas kernels: 5.81 us -> 8.85 us  [the longest x1 4.97 us: finish(): pl.pallas_call(functools.partial(finish_kernel, slot, first, count, n_col...]
    unnamed x32 -> x27, local copies, waits for them, and re-layouts: 8.3 us -> 10.8 us
  transfers between devices with their start and end apart: 21 -> 19, of which waited for: 13 -> 10; matrix products, arithmetic and copies ran while one was open for 11% -> 7% of each run, Pallas kernels for 15% -> 3%
where the time goes in v2:
time: 198 us
  blocking collectives  89.7 us (45%)
  Pallas kernels  31.9 us (16%)
  waiting for transfers between devices  27.4 us (14%)
  starting transfers between devices  23 us (12%)
  other arithmetic  13.3 us (7%)
  local copies, waits for them, and re-layouts  11 us (6%)
    all_to_all x2, blocking collectives, exchange(): return lax.all_to_all(x, BOTH, split_axis=0, concat_axis=0, tiled=True)  89.7 us
    ppermute x18, waiting for transfers between devices, swap(): lax.ppermute(x, axis, [(i, i ^ mask) for i in range(lax.axis_size(axis))])  27.4 us
    ppermute x18, starting transfers between devices, swap(): lax.ppermute(x, axis, [(i, i ^ mask) for i in range(lax.axis_size(axis))])  20.3 us
    pallas_call x1, Pallas kernels, region(): pl.pallas_call(functools.partial(region_kernel, n_row, n_col, chunks), ou...  17.8 us
    another operation x3, other arithmetic, body(): factor = lax.linalg.cholesky(pivot, symmetrize_input=False)  12.5 us
    unnamed x27, local copies, waits for them, and re-layouts  10.8 us
    pallas_call x1, Pallas kernels, finish(): pl.pallas_call(functools.partial(finish_kernel, slot, first, count, n_col...  4.97 us
  transfers between devices with their start and end apart: 19, of which 10 were waited for; matrix products, arithmetic and copies ran while one was open for 7% of the time, Pallas kernels for 3%

profile of v2, /device:TPU:0, one launch (start us, length us, event | category | flops | bytes accessed | tf_op | source)
XLA Modules:
  0.0 197.6 jit_solution(12134081715253675880)
XLA Ops:
  0.6 1.2 copy-done.5
  1.9 1.0 copy-done.7
  3.6 17.8 %region.1 = (f32[32,136,128]{2,1,0:T(8,128)S(1)}, f32[32,64,128]{2,1,0:T(8,128)S(1)}, f32[32,64,128]{2,1,0:T(8,128)S(1)}) custom-call(s32[8,8]{1,0:T(8,128)S(1)} %copy-done.11, bf16[8,512,1024]{2,1,0:T(8,128)(2,1)} %resid.1, bf16[8,512,128]{2,1,0:T(8,128)(2,1)S(1)} %copy-done.5, f32[8,128,128]{2,1,0:T(8,128)S(1)} %copy-done.7), custom_call_target="tpu_custom_call" | custom-call | tf_op jit(solution)/shard_map/region/pallas_call | solution.py:153
  21.4 34.7 %all_to_all.15.arrived = f32[32,64,128]{2,1,0:T(8,128)} all-to-all(f32[32,64,128]{2,1,0:T(8,128)S(1)} %get-tuple-element.19), channel_id=1, replica_groups=mesh['row'=4,'col'=8] {'row','col'}, dimensions={0} | all-to-all | bytes 2097152 | tf_op jit(solution)/shard_map/all_to_all | solution.py:426
  56.1 55.0 %all_to_all.16.arrived = f32[32,136,128]{2,1,0:T(8,128)S(1)} all-to-all(f32[32,136,128]{2,1,0:T(8,128)S(1)} %get-tuple-element.17), channel_id=1, replica_groups=mesh['row'=4,'col'=8] {'row','col'}, dimensions={0} | all-to-all | bytes 4456448 | tf_op jit(solution)/shard_map/all_to_all | solution.py:426
  111.1 2.8 %all-to-all-start.1 = ((f32[32,64,128]{2,1,0:T(8,128)}), f32[32,64,128]{2,1,0:T(8,128)S(1)}, u32[]{:S(2)}, u32[]{:S(2)}) async-start(f32[32,64,128]{2,1,0:T(8,128)} %copy-done.6), calls=%async_computation.1 | async-start | bytes 2097152 | tf_op jit(solution)/shard_map/all_to_all | solution.py:426
  114.2 1.9 first_tiles.1
  116.1 1.3 copy-done
  117.4 11.7 %cholesky.18 = f32[128,128]{1,0:T(8,128)S(1)} custom-call(f32[128,128]{1,0:T(8,128)S(1)} %get-tuple-element.21), custom_call_target="Cholesky" | custom-call | tf_op jit(solution)/shard_map/cholesky | solution.py:446
  130.5 2.5 %invert.1 = (f32[128,128]{1,0:T(8,128)S(1)}, f32[256,128]{1,0:T(8,128)S(1)}, f32[256,128]{1,0:T(8,128)S(1)}) custom-call(f32[128,128]{1,0:T(8,128)S(1)} %select_select_fusion.factor, f32[128,256]{1,0:T(8,128)S(1)} %copy-done.8), custom_call_target="tpu_custom_call" | custom-call | tf_op jit(solution)/shard_map/invert/pallas_call | solution.py:255
  133.0 2.7 %collective-permute-start.3 = (f32[256,128]{1,0:T(8,128)S(1)}, f32[256,128]{1,0:T(8,128)S(1)}, u32[]{:S(2)}, u32[]{:S(2)}) collective-permute-start(f32[256,128]{1,0:T(8,128)S(1)} %get-tuple-element.22.refs_0_), channel_id=1, source_target_pairs={{0,4},{1,5},{2,6},{3,7},{4,0},{5,1},{6,2},{7,3},{8,12},{9,13},{10,... | collective-permute-start | bytes 393224 | tf_op jit(solution)/shard_map/ppermute | solution.py:404
  135.7 2.4 %collective-permute-start.2 = (f32[256,128]{1,0:T(8,128)S(1)}, f32[256,128]{1,0:T(8,128)S(1)}, u32[]{:S(2)}, u32[]{:S(2)}) collective-permute-start(f32[256,128]{1,0:T(8,128)S(1)} %get-tuple-element.22.refs_0_), channel_id=1, source_target_pairs={{0,3},{1,2},{2,1},{3,0},{4,7},{5,6},{6,5},{7,4},{8,11},{9,10},{10,... | collective-permute-start | bytes 393224 | tf_op jit(solution)/shard_map/ppermute | solution.py:404
  139.2 6.5 %collective-permute-done.3.refs_4_ = f32[256,128]{1,0:T(8,128)S(1)} collective-permute-done((f32[256,128]{1,0:T(8,128)S(1)}, f32[256,128]{1,0:T(8,128)S(1)}, u32[]{:S(2)}, u32[]{:S(2)}) %collective-permute-start.3) | collective-permute-done | bytes 131104 | tf_op jit(solution)/shard_map/ppermute | solution.py:404
  145.7 3.0 %collective-permute-start.5 = (f32[256,128]{1,0:T(8,128)S(1)}, f32[256,128]{1,0:T(8,128)S(1)}, u32[]{:S(2)}, u32[]{:S(2)}) collective-permute-start(f32[256,128]{1,0:T(8,128)S(1)} %collective-permute-done.3.refs_4_), channel_id=1, source_target_pairs={{0,2},{1,3},{2,0},{3,1},{4,6},{5,7},{6,4},{7,5},{8,10},{9,11},{10,... | collective-permute-start | bytes 393224 | tf_op jit(solution)/shard_map/ppermute | solution.py:404
  149.2 1.6 copy-done.1
  150.8 1.2 copy-done.4
  152.0 1.4 more_tiles.1.total_in
  153.4 1.3 copy-done.2
  154.9 1.6 copy-done.3
  156.5 5.0 %finish.1 = (f32[8,1,128,512]{3,2,1,0:T(8,128)}, bf16[1024,512]{1,0:T(8,128)(2,1)S(1)}, bf16[1024,512]{1,0:T(8,128)(2,1)S(1)}, f32[2,256,128]{2,1,0:T(8,128)S(1)...) custom-call(s32[3]{0:T(128)S(1)} %copy-done.10, ...), custom_call_target="tpu_custom_call", output_to_operand_aliasing={{5}: (3, {})} | custom-call | tf_op jit(solution)/shard_map/finish/pallas_call | solution.py:350
  161.6 1.5 collective-permute-done.7
  163.1 1.6 collective-permute-start.8
  164.7 4.0 %collective-permute-done.8 = f32[1,256,128]{2,1,0:T(8,128)S(1)} collective-permute-done((f32[1,256,128]{2,1,0:T(8,128)S(1)}, f32[1,256,128]{2,1,0:T(8,128)S(1)}, u32[]{:S(2)}, u32[]{:S(2)}) %collective-permute-start.8) | collective-permute-done | bytes 131104 | tf_op jit(solution)/shard_map/ppermute | solution.py:404
  169.3 2.6 %collective-permute-start.11 = (f32[256,128]{1,0:T(8,128)S(1)}, f32[256,128]{1,0:T(8,128)S(1)}, u32[]{:S(2)}, u32[]{:S(2)}) collective-permute-start(f32[256,128]{1,0:T(8,128)S(1)} %fusion.refs_0_), channel_id=1, source_target_pairs={{0,3},{1,2},{2,1},{3,0},{4,7},{5,6},{6,5},{7,4},{8,11},{9,10},{10,... | collective-permute-start | bytes 393224 | tf_op jit(solution)/shard_map/ppermute | solution.py:404
  172.8 4.2 %collective-permute-done.12.refs_4_ = f32[256,128]{1,0:T(8,128)S(1)} collective-permute-done((f32[256,128]{1,0:T(8,128)S(1)}, f32[256,128]{1,0:T(8,128)S(1)}, u32[]{:S(2)}, u32[]{:S(2)}) %collective-permute-start.12) | collective-permute-done | bytes 131104 | tf_op jit(solution)/shard_map/ppermute | solution.py:404
  177.2 2.7 %collective-permute-start.14 = (f32[256,128]{1,0:T(8,128)S(1)}, f32[256,128]{1,0:T(8,128)S(1)}, u32[]{:S(2)}, u32[]{:S(2)}) collective-permute-start(f32[256,128]{1,0:T(8,128)S(1)} %collective-permute-done.12.refs_4_), channel_id=1, source_target_pairs={{0,2},{1,3},{2,0},{3,1},{4,6},{5,7},{6,4},{7,5},{8,10},{9,11},{10,... | collective-permute-start | bytes 393224 | tf_op jit(solution)/shard_map/ppermute | solution.py:404
  180.7 3.5 %collective-permute-done.15.refs_7_ = f32[256,128]{1,0:T(8,128)S(1)} collective-permute-done((f32[256,128]{1,0:T(8,128)S(1)}, f32[256,128]{1,0:T(8,128)S(1)}, u32[]{:S(2)}, u32[]{:S(2)}) %collective-permute-start.15) | collective-permute-done | bytes 131104 | tf_op jit(solution)/shard_map/ppermute | solution.py:404
  184.3 1.7 collective-permute-done.14.refs_6_
  186.0 3.3 %apply_matrix.1 = (f32[2,256,128]{2,1,0:T(8,128)S(1)}, f32[2,256,128]{2,1,0:T(8,128)S(1)}) custom-call(s32[3]{0:T(128)S(1)} %copy-done.10, bf16[1024,512]{1,0:T(8,128)(2,1)S(1)} %get-tuple-element.28.high, bf16[1024,512]{1,0:T(8,128)(2,1)S(1)} %get-tuple-element.29.low, f32[256,128]{1,0:T(8,128)S(1)} %fusion.refs_0_, ...), custom_call_target="tpu_custom_call" | custom-call | tf_op jit(solution)/shard_map/apply_matrix/pallas_call | solution.py:388
  189.4 1.5 collective-permute-done.16
  191.0 1.6 collective-permute-start.17
  192.6 4.0 %collective-permute-done.17 = f32[1,256,128]{2,1,0:T(8,128)S(1)} collective-permute-done((f32[1,256,128]{2,1,0:T(8,128)S(1)}, f32[1,256,128]{2,1,0:T(8,128)S(1)}, u32[]{:S(2)}, u32[]{:S(2)}) %collective-permute-start.17) | collective-permute-done | bytes 131104 | tf_op jit(solution)/shard_map/ppermute | solution.py:404
  (55 shorter events, 7.8 us)
Async XLA Ops:
  0.6 1.2 copy-start.5
  1.9 1.0 copy-start.7
  2.9 0.7 copy-start.11
  21.4 89.7 %copy-start.6 = (f32[32,64,128]{2,1,0:T(8,128)}, f32[32,64,128]{2,1,0:T(8,128)S(1)}, u32[]{:S(2)}) copy-start(f32[32,64,128]{2,1,0:T(8,128)S(1)} %get-tuple-element.18) | copy-start | bytes 3145732
  111.1 3.1 %copy-start.12 = (f32[128]{0:T(128)S(1)}, f32[128]{0:T(128)}, u32[]{:S(2)}) copy-start(f32[128]{0:T(128)} %param.11) | copy-start | bytes 1540
  111.1 19.4 %copy-start.8 = (f32[128,256]{1,0:T(8,128)S(1)}, f32[128,256]{1,0:T(8,128)}, u32[]{:S(2)}) copy-start(f32[128,256]{1,0:T(8,128)} %rhs.1) | copy-start | bytes 393220
  111.1 43.6 %all-to-all-start.1 = ((f32[32,64,128]{2,1,0:T(8,128)}), f32[32,64,128]{2,1,0:T(8,128)S(1)}, u32[]{:S(2)}, u32[]{:S(2)}) async-start(f32[32,64,128]{2,1,0:T(8,128)} %copy-done.6), calls=%async_computation.1 | async-start | bytes 2097152 | tf_op jit(solution)/shard_map/all_to_all | solution.py:426
  114.0 15.9 %copy-start.9 = (s32[3]{0:T(128)}, s32[3]{0:T(128)S(1)}, u32[]{:S(2)}) copy-start(s32[3]{0:T(128)S(1)} %pad_add_fusion.where) | copy-start | bytes 40
  116.1 1.3 copy-start
  133.0 12.7 %collective-permute-start.3 = (f32[256,128]{1,0:T(8,128)S(1)}, f32[256,128]{1,0:T(8,128)S(1)}, u32[]{:S(2)}, u32[]{:S(2)}) collective-permute-start(f32[256,128]{1,0:T(8,128)S(1)} %get-tuple-element.22.refs_0_), channel_id=1, source_target_pairs={{0,4},{1,5},{2,6},{3,7},{4,0},{5,1},{6,2},{7,3},{8,12},{9,13},{10,... | collective-permute-start | bytes 393224 | tf_op jit(solution)/shard_map/ppermute | solution.py:404
  135.7 13.0 %collective-permute-start.2 = (f32[256,128]{1,0:T(8,128)S(1)}, f32[256,128]{1,0:T(8,128)S(1)}, u32[]{:S(2)}, u32[]{:S(2)}) collective-permute-start(f32[256,128]{1,0:T(8,128)S(1)} %get-tuple-element.22.refs_0_), channel_id=1, source_target_pairs={{0,3},{1,2},{2,1},{3,0},{4,7},{5,6},{6,5},{7,4},{8,11},{9,10},{10,... | collective-permute-start | bytes 393224 | tf_op jit(solution)/shard_map/ppermute | solution.py:404
  138.2 16.6 %collective-permute-start.1 = (f32[256,128]{1,0:T(8,128)S(1)}, f32[256,128]{1,0:T(8,128)S(1)}, u32[]{:S(2)}, u32[]{:S(2)}) collective-permute-start(f32[256,128]{1,0:T(8,128)S(1)} %get-tuple-element.22.refs_0_), channel_id=1, source_target_pairs={{0,2},{1,3},{2,0},{3,1},{4,6},{5,7},{6,4},{7,5},{8,10},{9,11},{10,... | collective-permute-start | bytes 393224 | tf_op jit(solution)/shard_map/ppermute | solution.py:404
  138.7 16.1 %collective-permute-start = (f32[256,128]{1,0:T(8,128)S(1)}, f32[256,128]{1,0:T(8,128)S(1)}, u32[]{:S(2)}, u32[]{:S(2)}) collective-permute-start(f32[256,128]{1,0:T(8,128)S(1)} %get-tuple-element.22.refs_0_), channel_id=1, source_target_pairs={{0,1},{1,0},{2,3},{3,2},{4,5},{5,4},{6,7},{7,6},{8,9},{9,8},{10,11... | collective-permute-start | bytes 393224 | tf_op jit(solution)/shard_map/ppermute | solution.py:404
  145.7 9.1 %collective-permute-start.6 = (f32[256,128]{1,0:T(8,128)S(1)}, f32[256,128]{1,0:T(8,128)S(1)}, u32[]{:S(2)}, u32[]{:S(2)}) collective-permute-start(f32[256,128]{1,0:T(8,128)S(1)} %collective-permute-done.3.refs_4_), channel_id=1, source_target_pairs={{0,3},{1,2},{2,1},{3,0},{4,7},{5,6},{6,5},{7,4},{8,11},{9,10},{10,... | collective-permute-start | bytes 393224 | tf_op jit(solution)/shard_map/ppermute | solution.py:404
  145.7 9.2 %collective-permute-start.5 = (f32[256,128]{1,0:T(8,128)S(1)}, f32[256,128]{1,0:T(8,128)S(1)}, u32[]{:S(2)}, u32[]{:S(2)}) collective-permute-start(f32[256,128]{1,0:T(8,128)S(1)} %collective-permute-done.3.refs_4_), channel_id=1, source_target_pairs={{0,2},{1,3},{2,0},{3,1},{4,6},{5,7},{6,4},{7,5},{8,10},{9,11},{10,... | collective-permute-start | bytes 393224 | tf_op jit(solution)/shard_map/ppermute | solution.py:404
  148.7 6.2 %collective-permute-start.4 = (f32[256,128]{1,0:T(8,128)S(1)}, f32[256,128]{1,0:T(8,128)S(1)}, u32[]{:S(2)}, u32[]{:S(2)}) collective-permute-start(f32[256,128]{1,0:T(8,128)S(1)} %collective-permute-done.3.refs_4_), channel_id=1, source_target_pairs={{0,1},{1,0},{2,3},{3,2},{4,5},{5,4},{6,7},{7,6},{8,9},{9,8},{10,11... | collective-permute-start | bytes 393224 | tf_op jit(solution)/shard_map/ppermute | solution.py:404
  149.2 1.6 copy-start.1
  150.8 1.2 copy-start.4
  152.0 2.9 %copy-start.10 = (s32[3]{0:T(128)S(1)}, s32[3]{0:T(128)}, u32[]{:S(2)}) copy-start(s32[3]{0:T(128)} %copy-done.9) | copy-start | bytes 40
  153.4 1.3 copy-start.2
  154.9 1.6 copy-start.3
  161.5 1.6 collective-permute-start.7
  163.1 5.6 %collective-permute-start.8 = (f32[1,256,128]{2,1,0:T(8,128)S(1)}, f32[1,256,128]{2,1,0:T(8,128)S(1)}, u32[]{:S(2)}, u32[]{:S(2)}) collective-permute-start(f32[1,256,128]{2,1,0:T(8,128)S(1)} %slice.30), channel_id=1, source_target_pairs={{0,16},{8,24},{16,0},{24,8},{1,17},{9,25},{17,1},{25,9},{2,18},{10... | collective-permute-start | bytes 393224 | tf_op jit(solution)/shard_map/ppermute | solution.py:404
  169.0 8.0 %collective-permute-start.12 = (f32[256,128]{1,0:T(8,128)S(1)}, f32[256,128]{1,0:T(8,128)S(1)}, u32[]{:S(2)}, u32[]{:S(2)}) collective-permute-start(f32[256,128]{1,0:T(8,128)S(1)} %fusion.refs_0_), channel_id=1, source_target_pairs={{0,4},{1,5},{2,6},{3,7},{4,0},{5,1},{6,2},{7,3},{8,12},{9,13},{10,... | collective-permute-start | bytes 393224 | tf_op jit(solution)/shard_map/ppermute | solution.py:404
  169.3 10.5 %collective-permute-start.11 = (f32[256,128]{1,0:T(8,128)S(1)}, f32[256,128]{1,0:T(8,128)S(1)}, u32[]{:S(2)}, u32[]{:S(2)}) collective-permute-start(f32[256,128]{1,0:T(8,128)S(1)} %fusion.refs_0_), channel_id=1, source_target_pairs={{0,3},{1,2},{2,1},{3,0},{4,7},{5,6},{6,5},{7,4},{8,11},{9,10},{10,... | collective-permute-start | bytes 393224 | tf_op jit(solution)/shard_map/ppermute | solution.py:404
  172.0 8.7 %collective-permute-start.10 = (f32[256,128]{1,0:T(8,128)S(1)}, f32[256,128]{1,0:T(8,128)S(1)}, u32[]{:S(2)}, u32[]{:S(2)}) collective-permute-start(f32[256,128]{1,0:T(8,128)S(1)} %fusion.refs_0_), channel_id=1, source_target_pairs={{0,2},{1,3},{2,0},{3,1},{4,6},{5,7},{6,4},{7,5},{8,10},{9,11},{10,... | collective-permute-start | bytes 393224 | tf_op jit(solution)/shard_map/ppermute | solution.py:404
  172.1 8.7 %collective-permute-start.9 = (f32[256,128]{1,0:T(8,128)S(1)}, f32[256,128]{1,0:T(8,128)S(1)}, u32[]{:S(2)}, u32[]{:S(2)}) collective-permute-start(f32[256,128]{1,0:T(8,128)S(1)} %fusion.refs_0_), channel_id=1, source_target_pairs={{0,1},{1,0},{2,3},{3,2},{4,5},{5,4},{6,7},{7,6},{8,9},{9,8},{10,11... | collective-permute-start | bytes 393224 | tf_op jit(solution)/shard_map/ppermute | solution.py:404
  177.0 7.3 %collective-permute-start.15 = (f32[256,128]{1,0:T(8,128)S(1)}, f32[256,128]{1,0:T(8,128)S(1)}, u32[]{:S(2)}, u32[]{:S(2)}) collective-permute-start(f32[256,128]{1,0:T(8,128)S(1)} %collective-permute-done.12.refs_4_), channel_id=1, source_target_pairs={{0,3},{1,2},{2,1},{3,0},{4,7},{5,6},{6,5},{7,4},{8,11},{9,10},{10,... | collective-permute-start | bytes 393224 | tf_op jit(solution)/shard_map/ppermute | solution.py:404
  177.2 8.8 %collective-permute-start.14 = (f32[256,128]{1,0:T(8,128)S(1)}, f32[256,128]{1,0:T(8,128)S(1)}, u32[]{:S(2)}, u32[]{:S(2)}) collective-permute-start(f32[256,128]{1,0:T(8,128)S(1)} %collective-permute-done.12.refs_4_), channel_id=1, source_target_pairs={{0,2},{1,3},{2,0},{3,1},{4,6},{5,7},{6,4},{7,5},{8,10},{9,11},{10,... | collective-permute-start | bytes 393224 | tf_op jit(solution)/shard_map/ppermute | solution.py:404
  179.8 6.2 %collective-permute-start.13 = (f32[256,128]{1,0:T(8,128)S(1)}, f32[256,128]{1,0:T(8,128)S(1)}, u32[]{:S(2)}, u32[]{:S(2)}) collective-permute-start(f32[256,128]{1,0:T(8,128)S(1)} %collective-permute-done.12.refs_4_), channel_id=1, source_target_pairs={{0,1},{1,0},{2,3},{3,2},{4,5},{5,4},{6,7},{7,6},{8,9},{9,8},{10,11... | collective-permute-start | bytes 393224 | tf_op jit(solution)/shard_map/ppermute | solution.py:404
  189.3 1.6 collective-permute-start.16
  191.0 5.6 %collective-permute-start.17 = (f32[1,256,128]{2,1,0:T(8,128)S(1)}, f32[1,256,128]{2,1,0:T(8,128)S(1)}, u32[]{:S(2)}, u32[]{:S(2)}) collective-permute-start(f32[1,256,128]{2,1,0:T(8,128)S(1)} %slice.32), channel_id=1, source_target_pairs={{0,16},{8,24},{16,0},{24,8},{1,17},{9,25},{17,1},{25,9},{2,18},{10... | collective-permute-start | bytes 393224 | tf_op jit(solution)/shard_map/ppermute | solution.py:404

commit v3 on v2

--- a/solution.py
+++ b/solution.py
@@ -42,7 +42,7 @@
 def chunk_list(capacity):
     chunks = [(0, 0, PB + 8)]
     for slot in range(1, capacity):
-        chunks += [(slot, 0, PB // 2), (slot, PB // 2, PB // 2)]
+        chunks.append((slot, 0, PB))
     return chunks
 
 
@@ -173,7 +173,7 @@
             pltpu.SemaphoreType.DMA((3,)),
             pltpu.SemaphoreType.DMA((len(chunks),)),
         ],
-        compiler_params=params(48),
+        compiler_params=params(63),
         name="region",
     )(ids, resid, local, factor)
 
@@ -286,49 +286,75 @@
     )(places, arrived, total)
 
 
-def products(where, fetches, vectors, high, low, both, keep, away):
-    n_row = keep.shape[0] * 2
-    for mask, fetch in enumerate(fetches):
-        fetch.wait()
-        at = pl.multiple_of((where[2] ^ mask) * PB, PB)
-        vh, vl = split(vectors[mask])
+def half_product(where, side, vectors, high, low, both):
+    half = len(vectors)
+    for mask, vector in enumerate(vectors):
+        at = pl.multiple_of((lax.rem(where[2], half) ^ mask) * PB, PB)
+        vh, vl = split(vector[...])
         both[0, :, pl.ds(at, PB)] = vh
         both[1, :, pl.ds(at, PB)] = vl
-    result = dot_split((both[0], both[1]), (high[...], low[...]))
-    for sub in range(n_row):
-        mask = where[1] ^ sub
-        part = result[:, sub * PB : (sub + 1) * PB]
-
-        @pl.when(mask % 2 == 0)
-        def _():
-            keep[mask // 2] = part
-
-        @pl.when(mask % 2 == 1)
-        def _():
-            away[mask // 2] = part
-
-
-def fetch_all(sources, held, sem):
-    fetches = [pltpu.make_async_copy(x, held.at[i], sem.at[i]) for i, x in enumerate(sources)]
-    for fetch in fetches:
-        fetch.start()
-    return fetches
-
-
-def finish_kernel(slot, first, count, n_vec, where, places, arrived, total_in, *refs):
-    vectors = refs[:n_vec]
-    normal, high, low, keep, away, total, held, gathered, both, whole, in_sem, vec_sem, out_sem = (
-        refs[n_vec:]
-    )
-    n_row = keep.shape[0] * 2
-    fetches = fetch_all(vectors, gathered, vec_sem)
+    rows = pl.ds(pl.multiple_of((lax.div(where[2], half) ^ side) * (half * PB), half * PB), half * PB)
+    return dot_split((both[0], both[1]), (high[rows, :], low[rows, :]))
+
+
+def near_kernel(half, where, high, low, *refs):
+    vectors, (near, both) = refs[:half], refs[half:]
+    near[...] = half_product(where, 0, vectors, high, low, both)
+
+
+def far_kernel(half, where, near, high, low, *refs):
+    vectors, (keep, away, both) = refs[:half], refs[half:]
+    result = near[...] + half_product(where, 1, vectors, high, low, both)
+    odd = lax.rem(where[1], 2) == 1
+    for i in range(keep.shape[0]):
+        one = result[:, 2 * i * PB : (2 * i + 1) * PB]
+        two = result[:, (2 * i + 1) * PB : (2 * i + 2) * PB]
+        at = lax.div(where[1], 2) ^ i
+        keep[at] = jnp.where(odd, two, one)
+        away[at] = jnp.where(odd, one, two)
+
+
+def product_scratch(vectors):
+    return pltpu.VMEM((2, vectors[0].shape[0], len(vectors) * PB), jnp.bfloat16)
+
+
+def near_product(where, high, low, vectors):
+    return pl.pallas_call(
+        functools.partial(near_kernel, len(vectors)),
+        out_shape=jax.ShapeDtypeStruct((vectors[0].shape[0], high.shape[1]), jnp.float32),
+        in_specs=[SMEM, VMEM, VMEM] + [VMEM] * len(vectors),
+        out_specs=VMEM,
+        scratch_shapes=[product_scratch(vectors)],
+        compiler_params=params(12),
+        name="near_product",
+    )(where, high, low, *vectors)
+
+
+def far_product(where, near, high, low, vectors):
+    n_row = high.shape[1] // PB
+    halves = jax.ShapeDtypeStruct((n_row // 2, vectors[0].shape[0], PB), jnp.float32)
+    return pl.pallas_call(
+        functools.partial(far_kernel, len(vectors)),
+        out_shape=[halves, halves],
+        in_specs=[SMEM, VMEM, VMEM, VMEM] + [VMEM] * len(vectors),
+        out_specs=[VMEM] * 2,
+        scratch_shapes=[product_scratch(vectors)],
+        compiler_params=params(12),
+        name="far_product",
+    )(where, near, high, low, *vectors)
+
+
+def finish_kernel(slot, first, count, half, where, places, arrived, total_in, *refs):
+    vectors = refs[:half]
+    normal, high, low, near, total, held, both, whole, in_sem, out_sem = refs[half:]
+    n_col, n_row = whole.shape[0], whole.shape[2] // PB
     if count:
         fetch = pltpu.make_async_copy(arrived, held, in_sem)
         fetch.start()
         fetch.wait()
         add_tiles(places, slot, held, total, first, count)
     stores = []
-    for a in range(n_vec):
+    for a in range(n_col):
         for sub in range(n_row):
             tile = total[a * n_row + sub]
             whole[a, :, sub * PB : (sub + 1) * PB] = tile
@@ -337,67 +363,38 @@
             low[a * PB : (a + 1) * PB, sub * PB : (sub + 1) * PB] = tl
         stores.append(pltpu.make_async_copy(whole.at[a], normal.at[a, 0], out_sem.at[a]))
         stores[-1].start()
-    products(where, fetches, gathered, high, low, both, keep, away)
+    near[...] = half_product(where, 0, vectors, high, low, both)
     for store in stores:
         store.wait()
 
 
 def finish(where, places, arrived, total, vectors, n_row, slot, first, count):
-    n_col = len(vectors)
+    half = len(vectors)
+    n_col = 2 * half
     wide = vectors[0].shape[0]
-    halves = jax.ShapeDtypeStruct((n_row // 2, wide, PB), jnp.float32)
-    half = jax.ShapeDtypeStruct((n_col * PB, n_row * PB), jnp.bfloat16)
-    return pl.pallas_call(
-        functools.partial(finish_kernel, slot, first, count, n_col),
+    split_matrix = jax.ShapeDtypeStruct((n_col * PB, n_row * PB), jnp.bfloat16)
+    return pl.pallas_call(
+        functools.partial(finish_kernel, slot, first, count, half),
         out_shape=[
             jax.ShapeDtypeStruct((n_col, 1, PB, n_row * PB), jnp.float32),
-            half,
-            half,
-            halves,
-            halves,
+            split_matrix,
+            split_matrix,
+            jax.ShapeDtypeStruct((wide, n_row * PB), jnp.float32),
             jax.ShapeDtypeStruct(total.shape, jnp.float32),
         ],
-        in_specs=[SMEM, SMEM, ANY, VMEM] + [ANY] * n_col,
-        out_specs=[ANY] + [VMEM] * 5,
-        input_output_aliases={3: 5},
+        in_specs=[SMEM, SMEM, ANY, VMEM] + [VMEM] * half,
+        out_specs=[ANY] + [VMEM] * 4,
+        input_output_aliases={3: 4},
         scratch_shapes=[
             pltpu.VMEM(arrived.shape if count else (8, PB), jnp.float32),
-            pltpu.VMEM((n_col, wide, PB), jnp.float32),
-            pltpu.VMEM((2, wide, n_col * PB), jnp.bfloat16),
+            product_scratch(vectors),
             pltpu.VMEM((n_col, PB, n_row * PB), jnp.float32),
             pltpu.SemaphoreType.DMA,
             pltpu.SemaphoreType.DMA((n_col,)),
-            pltpu.SemaphoreType.DMA((n_col,)),
-        ],
-        compiler_params=params(32),
+        ],
+        compiler_params=params(24),
         name="finish",
     )(where, places, arrived, total, *vectors)
-
-
-def apply_kernel(n_vec, where, high, low, *refs):
-    vectors = refs[:n_vec]
-    keep, away, gathered, both, vec_sem = refs[n_vec:]
-    fetches = fetch_all(vectors, gathered, vec_sem)
-    products(where, fetches, gathered, high, low, both, keep, away)
-
-
-def apply_matrix(where, high, low, vectors, n_row):
-    n_col = len(vectors)
-    wide = vectors[0].shape[0]
-    halves = jax.ShapeDtypeStruct((n_row // 2, wide, PB), jnp.float32)
-    return pl.pallas_call(
-        functools.partial(apply_kernel, n_col),
-        out_shape=[halves, halves],
-        in_specs=[SMEM, VMEM, VMEM] + [ANY] * n_col,
-        out_specs=[VMEM] * 2,
-        scratch_shapes=[
-            pltpu.VMEM((n_col, wide, PB), jnp.float32),
-            pltpu.VMEM((2, wide, n_col * PB), jnp.bfloat16),
-            pltpu.SemaphoreType.DMA((n_col,)),
-        ],
-        compiler_params=params(12),
-        name="apply_matrix",
-    )(where, high, low, *vectors)
 
 
 def swap(x, axis, mask):
@@ -409,7 +406,7 @@
     far = swap(own, "col", half)
     near = [own] + [swap(own, "col", mask) for mask in range(1, half)]
     beyond = [far] + [swap(far, "col", mask) for mask in range(1, half)]
-    return near + beyond
+    return near, beyond
 
 
 def sum_rows(keep, away):
@@ -445,15 +442,16 @@
     total, pivot = first_tiles(where, places, arrived[0], damping[None, :], devices)
     factor = lax.linalg.cholesky(pivot, symmetrize_input=False)
     inverse, residual, update = invert(factor, right_sides)
-    vectors = gather_columns(update)
+    close, beyond = gather_columns(update)
 
     for (slot, first, count), x in list(zip(chunks, arrived))[1:-1]:
         total = more_tiles(places, x, total, slot, first, count)
     slot, first, count = chunks[-1]
-    normal, high, low, keep, away, _ = finish(
-        where, places, arrived[-1], total, vectors, n_row, slot, first, count if slot else 0
+    normal, high, low, near, _ = finish(
+        where, places, arrived[-1], total, close, n_row, slot, first, count if slot else 0
     )
     high_dot = functools.partial(jnp.dot, precision=lax.Precision.HIGHEST)
+    keep, away = far_product(where, near, high, low, beyond)
     answer = update
     weight = 1.0 / ratio
     for sweep in range(1, ITERS):
@@ -465,8 +463,9 @@
         weight = weight_next
         answer = answer + update
         if sweep + 1 < ITERS:
-            vectors = gather_columns(update)
-            keep, away = apply_matrix(where, high, low, vectors, n_row)
+            close, beyond = gather_columns(update)
+            near = near_product(where, high, low, close)
+            keep, away = far_product(where, near, high, low, beyond)
     return normal, answer.T
 
 

time: 198 us -> 186 us (0.939)
  blocking collectives: 89.7 us -> 60.1 us
  waiting for transfers between devices: 27.4 us -> 48.7 us
  local copies, waits for them, and re-layouts: 11 us -> 3.85 us
  Pallas kernels: 31.9 us -> 34.6 us
    all_to_all x2 -> x1, blocking collectives: 89.7 us -> 60.1 us  [exchange(): return lax.all_to_all(x, BOTH, split_axis=0, concat_axis=0, tiled=True)]
    ppermute x18, waiting for transfers between devices: 27.4 us -> 48.7 us  [swap(): lax.ppermute(x, axis, [(i, i ^ mask) for i in range(lax.axis_size(axis))])]
    unnamed x27 -> x9, local copies, waits for them, and re-layouts: 10.8 us -> 3.65 us
    pallas_call x1, Pallas kernels: 17.8 us -> 21.3 us  [region(): pl.pallas_call(functools.partial(region_kernel, n_row, n_col, chunks), ou...]
    pallas_call x3 -> x4, Pallas kernels: 9.71 us -> 8.89 us  [the longest x1 5.24 us: finish(): pl.pallas_call(functools.partial(finish_kernel, slot, first, count, half)...]
  transfers between devices with their start and end apart: 19 -> 19, of which waited for: 10 -> 9; matrix products, arithmetic and copies ran while one was open for 7% -> 7% of each run, Pallas kernels for 3% -> 6%
where the time goes in v3:
time: 186 us; the launch traced here: 185 us
  blocking collectives  60.1 us (32%)
  waiting for transfers between devices  48.7 us (26%)
  Pallas kernels  34.6 us (19%)
  starting transfers between devices  23.7 us (13%)
  other arithmetic  13.2 us (7%)
  local copies, waits for them, and re-layouts  3.85 us (2%)
    all_to_all x1, blocking collectives, exchange(): return lax.all_to_all(x, BOTH, split_axis=0, concat_axis=0, tiled=True)  60.1 us
    ppermute x18, waiting for transfers between devices, swap(): lax.ppermute(x, axis, [(i, i ^ mask) for i in range(lax.axis_size(axis))])  48.7 us
    pallas_call x1, Pallas kernels, region(): pl.pallas_call(functools.partial(region_kernel, n_row, n_col, chunks), ou...  21.3 us
    ppermute x18, starting transfers between devices, swap(): lax.ppermute(x, axis, [(i, i ^ mask) for i in range(lax.axis_size(axis))])  20 us
    another operation x3, other arithmetic, body(): factor = lax.linalg.cholesky(pivot, symmetrize_input=False)  12.4 us
    pallas_call x1, Pallas kernels, finish(): pl.pallas_call(functools.partial(finish_kernel, slot, first, count, half)...  5.24 us
  transfers between devices with their start and end apart: 19, of which 9 were waited for; matrix products, arithmetic and copies ran while one was open for 7% of the time, Pallas kernels for 6%

profile of v3, /device:TPU:0, one launch (start us, length us, event | category | flops | bytes accessed | tf_op | source)
XLA Modules:
  0.0 185.5 jit_solution(16585342230970161139)
XLA Ops:
  0.6 21.3 %region.1 = (f32[32,136,128]{2,1,0:T(8,128)}, f32[32,128,128]{2,1,0:T(8,128)}) custom-call(s32[8,8]{1,0:T(8,128)} %ids_in.1, bf16[8,512,1024]{2,1,0:T(8,128)(2,1)} %resid.1, bf16[8,512,128]{2,1,0:T(8,128)(2,1)} %local_in.1, f32[8,128,128]{2,1,0:T(8,128)} %factor_in.1), custom_call_target="tpu_custom_call" | custom-call | tf_op jit(solution)/shard_map/region/pallas_call | solution.py:153
  21.9 60.1 %all_to_all.10.arrived = f32[32,136,128]{2,1,0:T(8,128)S(1)} all-to-all(f32[32,136,128]{2,1,0:T(8,128)} %get-tuple-element.17), channel_id=1, replica_groups=mesh['row'=4,'col'=8] {'row','col'}, dimensions={0} | all-to-all | bytes 4456448 | tf_op jit(solution)/shard_map/all_to_all | solution.py:423
  82.0 3.6 %all-to-all-start.1 = ((f32[32,128,128]{2,1,0:T(8,128)}), f32[32,128,128]{2,1,0:T(8,128)}, u32[]{:S(2)}, u32[]{:S(2)}) async-start(f32[32,128,128]{2,1,0:T(8,128)} %get-tuple-element.18), calls=%async_computation.1 | async-start | bytes 4194304 | tf_op jit(solution)/shard_map/all_to_all | solution.py:423
  85.9 1.9 %first_tiles.1 = (f32[32,128,128]{2,1,0:T(8,128)S(1)}, f32[128,128]{1,0:T(8,128)S(1)}) custom-call(s32[3]{0:T(128)S(1)} %pad_add_fusion.where, s32[32,2]{1,0:T(8,128)S(1)} %copy.15.places, f32[32,136,128]{2,1,0:T(8,128)S(1)} %all_to_all.10.arrived, f32[1,128]{1,0:T(1,128)S(1)} %bitcast.24), custom_call_target="tpu_custom_call" | custom-call | tf_op jit(solution)/shard_map/first_tiles/pallas_call | solution.py:208
  87.8 1.3 copy-done
  89.1 11.7 %cholesky.18 = f32[128,128]{1,0:T(8,128)S(1)} custom-call(f32[128,128]{1,0:T(8,128)S(1)} %get-tuple-element.20), custom_call_target="Cholesky" | custom-call | tf_op jit(solution)/shard_map/cholesky | solution.py:443
  102.2 2.5 %invert.1 = (f32[128,128]{1,0:T(8,128)S(1)}, f32[256,128]{1,0:T(8,128)S(1)}, f32[256,128]{1,0:T(8,128)S(1)}) custom-call(f32[128,128]{1,0:T(8,128)S(1)} %select_select_fusion.factor, f32[128,256]{1,0:T(8,128)S(1)} %copy-done.2), custom_call_target="tpu_custom_call" | custom-call | tf_op jit(solution)/shard_map/invert/pallas_call | solution.py:255
  104.7 2.6 %collective-permute-start.3 = (f32[256,128]{1,0:T(8,128)S(1)}, f32[256,128]{1,0:T(8,128)S(1)}, u32[]{:S(2)}, u32[]{:S(2)}) collective-permute-start(f32[256,128]{1,0:T(8,128)S(1)} %get-tuple-element.21.refs_0_), channel_id=1, source_target_pairs={{0,4},{1,5},{2,6},{3,7},{4,0},{5,1},{6,2},{7,3},{8,12},{9,13},{10,... | collective-permute-start | bytes 393224 | tf_op jit(solution)/shard_map/ppermute | solution.py:401
  107.3 1.5 collective-permute-start
  108.8 1.5 collective-permute-start.1
  110.8 28.9 %collective-permute-done.3.refs_0_ = f32[256,128]{1,0:T(8,128)S(1)} collective-permute-done((f32[256,128]{1,0:T(8,128)S(1)}, f32[256,128]{1,0:T(8,128)S(1)}, u32[]{:S(2)}, u32[]{:S(2)}) %collective-permute-start.3) | collective-permute-done | bytes 131104 | tf_op jit(solution)/shard_map/ppermute | solution.py:401
  139.8 1.5 collective-permute-start.4
  141.3 2.0 %collective-permute-start.6 = (f32[256,128]{1,0:T(8,128)S(1)}, f32[256,128]{1,0:T(8,128)S(1)}, u32[]{:S(2)}, u32[]{:S(2)}) collective-permute-start(f32[256,128]{1,0:T(8,128)S(1)} %collective-permute-done.3.refs_0_), channel_id=1, source_target_pairs={{0,3},{1,2},{2,1},{3,0},{4,7},{5,6},{6,5},{7,4},{8,11},{9,10},{10,... | collective-permute-start | bytes 393224 | tf_op jit(solution)/shard_map/ppermute | solution.py:401
  143.3 1.6 copy-done.1
  144.9 5.2 %finish.1 = (f32[8,1,128,512]{3,2,1,0:T(8,128)}, bf16[1024,512]{1,0:T(8,128)(2,1)S(1)}, bf16[1024,512]{1,0:T(8,128)(2,1)S(1)}, f32[256,512]{1,0:T(8,128)S(1)}, f32[32,128,128]{2,1,0:T(8,128)S(1)}) custom-call(s32[3]{0:T(128)S(1)} %pad_add_fusion.where, s32[32,2]{1,0:T(8,128)S(1)} %copy.15.places, ...), custom_call_target="tpu_custom_call", output_to_operand_aliasing={{4}: (3, {})} | custom-call | tf_op jit(solution)/shard_map/finish/pallas_call | solution.py:376
  150.2 1.2 far_product.2
  151.5 1.5 collective-permute-done.7
  153.0 1.6 collective-permute-start.8
  154.6 4.0 %collective-permute-done.8 = f32[1,256,128]{2,1,0:T(8,128)S(1)} collective-permute-done((f32[1,256,128]{2,1,0:T(8,128)S(1)}, f32[1,256,128]{2,1,0:T(8,128)S(1)}, u32[]{:S(2)}, u32[]{:S(2)}) %collective-permute-start.8) | collective-permute-done | bytes 131104 | tf_op jit(solution)/shard_map/ppermute | solution.py:401
  159.1 1.7 collective-permute-start.10
  160.9 1.2 collective-permute-start.11
  162.6 4.2 %collective-permute-done.12.refs_0_ = f32[256,128]{1,0:T(8,128)S(1)} collective-permute-done((f32[256,128]{1,0:T(8,128)S(1)}, f32[256,128]{1,0:T(8,128)S(1)}, u32[]{:S(2)}, u32[]{:S(2)}) %collective-permute-start.12) | collective-permute-done | bytes 131104 | tf_op jit(solution)/shard_map/ppermute | solution.py:401
  166.8 1.4 collective-permute-start.13
  168.3 2.0 %collective-permute-start.15 = (f32[256,128]{1,0:T(8,128)S(1)}, f32[256,128]{1,0:T(8,128)S(1)}, u32[]{:S(2)}, u32[]{:S(2)}) collective-permute-start(f32[256,128]{1,0:T(8,128)S(1)} %collective-permute-done.12.refs_0_), channel_id=1, source_target_pairs={{0,3},{1,2},{2,1},{3,0},{4,7},{5,6},{6,5},{7,4},{8,11},{9,10},{10,... | collective-permute-start | bytes 393224 | tf_op jit(solution)/shard_map/ppermute | solution.py:401
  170.5 1.2 near_product.1.near
  171.7 2.9 %collective-permute-done.13.refs_1_ = f32[256,128]{1,0:T(8,128)S(1)} collective-permute-done((f32[256,128]{1,0:T(8,128)S(1)}, f32[256,128]{1,0:T(8,128)S(1)}, u32[]{:S(2)}, u32[]{:S(2)}) %collective-permute-start.13) | collective-permute-done | bytes 131104 | tf_op jit(solution)/shard_map/ppermute | solution.py:401
  174.5 1.4 collective-permute-done.15.refs_3_
  175.9 1.2 far_product.3
  177.3 1.5 collective-permute-done.16
  178.8 1.5 collective-permute-start.17
  180.3 4.1 %collective-permute-done.17 = f32[1,256,128]{2,1,0:T(8,128)S(1)} collective-permute-done((f32[1,256,128]{2,1,0:T(8,128)S(1)}, f32[1,256,128]{2,1,0:T(8,128)S(1)}, u32[]{:S(2)}, u32[]{:S(2)}) %collective-permute-start.17) | collective-permute-done | bytes 131104 | tf_op jit(solution)/shard_map/ppermute | solution.py:401
  184.7 0.8 copy.16
  (37 shorter events, 3.8 us)
Async XLA Ops:
  82.0 3.9 %copy-start.3 = (f32[128]{0:T(128)S(1)}, f32[128]{0:T(128)}, u32[]{:S(2)}) copy-start(f32[128]{0:T(128)} %param.11) | copy-start | bytes 1540
  82.0 61.3 %all-to-all-start.1 = ((f32[32,128,128]{2,1,0:T(8,128)}), f32[32,128,128]{2,1,0:T(8,128)}, u32[]{:S(2)}, u32[]{:S(2)}) async-start(f32[32,128,128]{2,1,0:T(8,128)} %get-tuple-element.18), calls=%async_computation.1 | async-start | bytes 4194304 | tf_op jit(solution)/shard_map/all_to_all | solution.py:423
  85.6 16.6 %copy-start.2 = (f32[128,256]{1,0:T(8,128)S(1)}, f32[128,256]{1,0:T(8,128)}, u32[]{:S(2)}) copy-start(f32[128,256]{1,0:T(8,128)} %rhs.1) | copy-start | bytes 393220
  87.8 1.3 copy-start
  104.7 35.1 %collective-permute-start.3 = (f32[256,128]{1,0:T(8,128)S(1)}, f32[256,128]{1,0:T(8,128)S(1)}, u32[]{:S(2)}, u32[]{:S(2)}) collective-permute-start(f32[256,128]{1,0:T(8,128)S(1)} %get-tuple-element.21.refs_0_), channel_id=1, source_target_pairs={{0,4},{1,5},{2,6},{3,7},{4,0},{5,1},{6,2},{7,3},{8,12},{9,13},{10,... | collective-permute-start | bytes 393224 | tf_op jit(solution)/shard_map/ppermute | solution.py:401
  107.3 33.9 %collective-permute-start = (f32[256,128]{1,0:T(8,128)S(1)}, f32[256,128]{1,0:T(8,128)S(1)}, u32[]{:S(2)}, u32[]{:S(2)}) collective-permute-start(f32[256,128]{1,0:T(8,128)S(1)} %get-tuple-element.21.refs_0_), channel_id=1, source_target_pairs={{0,1},{1,0},{2,3},{3,2},{4,5},{5,4},{6,7},{7,6},{8,9},{9,8},{10,11... | collective-permute-start | bytes 393224 | tf_op jit(solution)/shard_map/ppermute | solution.py:401
  108.8 34.5 %collective-permute-start.1 = (f32[256,128]{1,0:T(8,128)S(1)}, f32[256,128]{1,0:T(8,128)S(1)}, u32[]{:S(2)}, u32[]{:S(2)}) collective-permute-start(f32[256,128]{1,0:T(8,128)S(1)} %get-tuple-element.21.refs_0_), channel_id=1, source_target_pairs={{0,2},{1,3},{2,0},{3,1},{4,6},{5,7},{6,4},{7,5},{8,10},{9,11},{10,... | collective-permute-start | bytes 393224 | tf_op jit(solution)/shard_map/ppermute | solution.py:401
  110.4 32.9 %collective-permute-start.2 = (f32[256,128]{1,0:T(8,128)S(1)}, f32[256,128]{1,0:T(8,128)S(1)}, u32[]{:S(2)}, u32[]{:S(2)}) collective-permute-start(f32[256,128]{1,0:T(8,128)S(1)} %get-tuple-element.21.refs_0_), channel_id=1, source_target_pairs={{0,3},{1,2},{2,1},{3,0},{4,7},{5,6},{6,5},{7,4},{8,11},{9,10},{10,... | collective-permute-start | bytes 393224 | tf_op jit(solution)/shard_map/ppermute | solution.py:401
  139.8 10.4 %collective-permute-start.4 = (f32[256,128]{1,0:T(8,128)S(1)}, f32[256,128]{1,0:T(8,128)S(1)}, u32[]{:S(2)}, u32[]{:S(2)}) collective-permute-start(f32[256,128]{1,0:T(8,128)S(1)} %collective-permute-done.3.refs_0_), channel_id=1, source_target_pairs={{0,1},{1,0},{2,3},{3,2},{4,5},{5,4},{6,7},{7,6},{8,9},{9,8},{10,11... | collective-permute-start | bytes 393224 | tf_op jit(solution)/shard_map/ppermute | solution.py:401
  141.3 8.9 %collective-permute-start.5 = (f32[256,128]{1,0:T(8,128)S(1)}, f32[256,128]{1,0:T(8,128)S(1)}, u32[]{:S(2)}, u32[]{:S(2)}) collective-permute-start(f32[256,128]{1,0:T(8,128)S(1)} %collective-permute-done.3.refs_0_), channel_id=1, source_target_pairs={{0,2},{1,3},{2,0},{3,1},{4,6},{5,7},{6,4},{7,5},{8,10},{9,11},{10,... | collective-permute-start | bytes 393224 | tf_op jit(solution)/shard_map/ppermute | solution.py:401
  141.3 8.9 %collective-permute-start.6 = (f32[256,128]{1,0:T(8,128)S(1)}, f32[256,128]{1,0:T(8,128)S(1)}, u32[]{:S(2)}, u32[]{:S(2)}) collective-permute-start(f32[256,128]{1,0:T(8,128)S(1)} %collective-permute-done.3.refs_0_), channel_id=1, source_target_pairs={{0,3},{1,2},{2,1},{3,0},{4,7},{5,6},{6,5},{7,4},{8,11},{9,10},{10,... | collective-permute-start | bytes 393224 | tf_op jit(solution)/shard_map/ppermute | solution.py:401
  143.3 1.6 copy-start.1
  151.4 1.6 collective-permute-start.7
  153.0 5.6 %collective-permute-start.8 = (f32[1,256,128]{2,1,0:T(8,128)S(1)}, f32[1,256,128]{2,1,0:T(8,128)S(1)}, u32[]{:S(2)}, u32[]{:S(2)}) collective-permute-start(f32[1,256,128]{2,1,0:T(8,128)S(1)} %slice.30), channel_id=1, source_target_pairs={{0,16},{8,24},{16,0},{24,8},{1,17},{9,25},{17,1},{25,9},{2,18},{10... | collective-permute-start | bytes 393224 | tf_op jit(solution)/shard_map/ppermute | solution.py:401
  158.9 7.9 %collective-permute-start.12 = (f32[256,128]{1,0:T(8,128)S(1)}, f32[256,128]{1,0:T(8,128)S(1)}, u32[]{:S(2)}, u32[]{:S(2)}) collective-permute-start(f32[256,128]{1,0:T(8,128)S(1)} %fusion.refs_0_), channel_id=1, source_target_pairs={{0,4},{1,5},{2,6},{3,7},{4,0},{5,1},{6,2},{7,3},{8,12},{9,13},{10,... | collective-permute-start | bytes 393224 | tf_op jit(solution)/shard_map/ppermute | solution.py:401
  159.1 9.2 %collective-permute-start.10 = (f32[256,128]{1,0:T(8,128)S(1)}, f32[256,128]{1,0:T(8,128)S(1)}, u32[]{:S(2)}, u32[]{:S(2)}) collective-permute-start(f32[256,128]{1,0:T(8,128)S(1)} %fusion.refs_0_), channel_id=1, source_target_pairs={{0,2},{1,3},{2,0},{3,1},{4,6},{5,7},{6,4},{7,5},{8,10},{9,11},{10,... | collective-permute-start | bytes 393224 | tf_op jit(solution)/shard_map/ppermute | solution.py:401
  160.9 9.6 %collective-permute-start.11 = (f32[256,128]{1,0:T(8,128)S(1)}, f32[256,128]{1,0:T(8,128)S(1)}, u32[]{:S(2)}, u32[]{:S(2)}) collective-permute-start(f32[256,128]{1,0:T(8,128)S(1)} %fusion.refs_0_), channel_id=1, source_target_pairs={{0,3},{1,2},{2,1},{3,0},{4,7},{5,6},{6,5},{7,4},{8,11},{9,10},{10,... | collective-permute-start | bytes 393224 | tf_op jit(solution)/shard_map/ppermute | solution.py:401
  162.1 8.4 %collective-permute-start.9 = (f32[256,128]{1,0:T(8,128)S(1)}, f32[256,128]{1,0:T(8,128)S(1)}, u32[]{:S(2)}, u32[]{:S(2)}) collective-permute-start(f32[256,128]{1,0:T(8,128)S(1)} %fusion.refs_0_), channel_id=1, source_target_pairs={{0,1},{1,0},{2,3},{3,2},{4,5},{5,4},{6,7},{7,6},{8,9},{9,8},{10,11... | collective-permute-start | bytes 393224 | tf_op jit(solution)/shard_map/ppermute | solution.py:401
  166.8 7.7 %collective-permute-start.13 = (f32[256,128]{1,0:T(8,128)S(1)}, f32[256,128]{1,0:T(8,128)S(1)}, u32[]{:S(2)}, u32[]{:S(2)}) collective-permute-start(f32[256,128]{1,0:T(8,128)S(1)} %collective-permute-done.12.refs_0_), channel_id=1, source_target_pairs={{0,1},{1,0},{2,3},{3,2},{4,5},{5,4},{6,7},{7,6},{8,9},{9,8},{10,11... | collective-permute-start | bytes 393224 | tf_op jit(solution)/shard_map/ppermute | solution.py:401
  168.3 6.2 %collective-permute-start.14 = (f32[256,128]{1,0:T(8,128)S(1)}, f32[256,128]{1,0:T(8,128)S(1)}, u32[]{:S(2)}, u32[]{:S(2)}) collective-permute-start(f32[256,128]{1,0:T(8,128)S(1)} %collective-permute-done.12.refs_0_), channel_id=1, source_target_pairs={{0,2},{1,3},{2,0},{3,1},{4,6},{5,7},{6,4},{7,5},{8,10},{9,11},{10,... | collective-permute-start | bytes 393224 | tf_op jit(solution)/shard_map/ppermute | solution.py:401
  168.3 7.6 %collective-permute-start.15 = (f32[256,128]{1,0:T(8,128)S(1)}, f32[256,128]{1,0:T(8,128)S(1)}, u32[]{:S(2)}, u32[]{:S(2)}) collective-permute-start(f32[256,128]{1,0:T(8,128)S(1)} %collective-permute-done.12.refs_0_), channel_id=1, source_target_pairs={{0,3},{1,2},{2,1},{3,0},{4,7},{5,6},{6,5},{7,4},{8,11},{9,10},{10,... | collective-permute-start | bytes 393224 | tf_op jit(solution)/shard_map/ppermute | solution.py:401
  177.2 1.6 collective-permute-start.16
  178.8 5.6 %collective-permute-start.17 = (f32[1,256,128]{2,1,0:T(8,128)S(1)}, f32[1,256,128]{2,1,0:T(8,128)S(1)}, u32[]{:S(2)}, u32[]{:S(2)}) collective-permute-start(f32[1,256,128]{2,1,0:T(8,128)S(1)} %slice.32), channel_id=1, source_target_pairs={{0,16},{8,24},{16,0},{24,8},{1,17},{9,25},{17,1},{25,9},{2,18},{10... | collective-permute-start | bytes 393224 | tf_op jit(solution)/shard_map/ppermute | solution.py:401
